TPU v7x, 512 devices: a whole 4x4x16 slice. The times are simulated.
512 devices in a mesh: dp: 32 (over z_lo, x, core), tensor: 16 (over z_hi, y).
Axes of the slice: x: 4, y: 4, z: 16 (z_hi: 4, z_lo: 4; z = z_hi * 4 + z_lo), core: 2. Of those that a mesh axis runs over, the one named last changes fastest.
Arguments:
- inputs: bfloat16 [32768, 8192], P('dp', 'tensor'), may hold values from -6 to 6
- cotangent: bfloat16 [32768, 8192], P('dp', 'tensor'), may hold values from -6 to 6
- projector: bfloat16 [8192, 512], P('tensor'), may hold values from -0.0625 to 0.0625
- weight: bfloat16 [8192, 8192], P('dp', 'tensor'), may hold values from -6 to 6
- moment: float32 [512, 8192], P('dp', 'tensor'), may hold values from -6 to 6
- second_moment: float32 [512, 8192], P('dp', 'tensor'), may hold values from 0.01 to 1
Outputs:
- new_weight: bfloat16 [8192, 8192], P('dp', 'tensor')
- new_moment: float32 [512, 8192], P('dp', 'tensor')
- new_second: float32 [512, 8192], P('dp', 'tensor')
All inputs are finite; a program needn't handle non-finite values.
Results may differ from a plain program's by a relative error of at most 0.0034.
Values may be sent and summed in bfloat16 or wider, within the bound.
No kernel may reach another device: no remote copies, remote signals or barrier semaphores. Data moves between devices by JAX's collectives and lax.ppermute only.
A program may use at most 64 MiB of HBM per device.

v0:
```python
import math

import jax
import jax.numpy as jnp
from jax import lax
from jax.sharding import PartitionSpec as P

STEP = 1000


beta_one = 0.9
beta_two = 0.999
epsilon = 1e-08
step_size = 0.5


def broadcast(value, axis, source):
    kept = jnp.where(lax.axis_index(axis) == source, value, 0).astype(value.dtype)
    return lax.psum(kept, axis)


def on_device(inputs, cotangent, projector, weight, moment, second_moment):
    tensor_count = lax.axis_size("tensor")
    data_count = lax.axis_size("dp")
    partial_sum = jnp.dot(inputs, projector, preferred_element_type=jnp.float32)
    projected = lax.psum(partial_sum, "tensor").astype(jnp.bfloat16)
    scale = 1.0 / math.sqrt(inputs.shape[0] * data_count)
    columns = projected
    gradient = (
        lax.psum_scatter(
            lax.dot_general(
                columns, cotangent, (((0,), (0,)), ((), ())), preferred_element_type=jnp.float32
            ),
            "dp",
            scatter_dimension=0,
            tiled=True,
        )
        * scale
    )
    new_moment = beta_one * moment + (1.0 - beta_one) * gradient
    new_second = beta_two * second_moment + (1.0 - beta_two) * gradient * gradient
    first_fix = 1.0 - beta_one**STEP
    second_fix = 1.0 - beta_two**STEP
    update = (new_moment / first_fix / (jnp.sqrt(new_second / second_fix) + epsilon)).astype(
        jnp.bfloat16
    )
    row_count = weight.shape[0]
    ratio = data_count // tensor_count
    data_index = lax.axis_index("dp")
    source = data_index // ratio
    block = broadcast(projector, "tensor", source)
    own_rows = lax.dynamic_slice_in_dim(block, data_index % ratio * row_count, row_count, 0)
    initial = jnp.zeros((row_count, weight.shape[1]), jnp.float32)
    segment = lax.all_gather(update, "dp", axis=0, tiled=True)
    columns = lax.slice_in_dim(own_rows, 0, segment.shape[0], axis=1)
    expanded = initial + jnp.dot(columns, segment, preferred_element_type=jnp.float32)
    new_weight = (weight.astype(jnp.float32) - step_size * expanded).astype(jnp.bfloat16)
    return (new_weight, new_moment, new_second)


def solution(mesh):
    return jax.shard_map(
        on_device,
        mesh=mesh,
        in_specs=(
            P("dp", "tensor"),
            P("dp", "tensor"),
            P("tensor", None),
            P("dp", "tensor"),
            P("dp", "tensor"),
            P("dp", "tensor"),
        ),
        out_specs=(P("dp", "tensor"), P("dp", "tensor"), P("dp", "tensor")),
        check_vma=False,
    )
```

profile of v0, /device:TPU:6, one launch (start us, length us, event | category | flops | bytes accessed | tf_op | source)
XLA Modules:
  0.0 445.6 jit_solution(7771616963355561387)
XLA Ops:
  8.0 0.0 copy-start
  8.0 0.0 reduce-scatter.2.cloned.1.call-start
  8.1 1.2 copy-done
  9.2 1.7 fusion.6
  11.0 204.3 %all-reduce.4 = bf16[1024,512]{1,0:T(8,128)(2,1)} all-reduce(f32[1024,512]{1,0:T(8,128)S(1)} %fusion.6), channel_id=1, replica_groups=mesh['dp'=32,'tensor'=16] {'tensor'}, use_global_device_ids=true, to_apply=%region_1.0 | all-reduce | flops 524288 | bytes 3145728 | tf_op jit(solution)/shard_map/psum | solution.py:26
  215.3 0.0 copy-start.1
  215.3 3.3 fusion.7
  218.6 0.0 copy-start.3
  218.6 0.0 copy-start.4
  218.6 0.0 copy-start.2
  218.6 0.0 reduce-scatter.2.cloned.1.call-update
  218.6 0.0 all-reduce.3.cloned.1.call-start
  218.6 0.0 copy-done.1
  218.7 0.8 broadcast_select_fusion
  219.5 0.0 all-reduce.3.cloned.1.call-update
  219.5 144.8 %reduce-scatter.2.cloned.1.call-done = f32[16,512]{1,0:T(8,128)} async-done(((f32[512,512]{1,0:T(8,128)}), f32[16,512]{1,0:T(8,128)}) %reduce-scatter.2.cloned.1.call-update) | async-done | bytes 32784 | tf_op jit(solution)/shard_map/reduce_scatter | solution.py:30
  364.3 0.0 copy-done.3
  364.3 0.0 copy-done.4
  364.3 1.4 divide_convert_fusion
  365.7 52.3 %all_gather.3 = bf16[512,512]{1,0:T(8,128)(2,1)S(1)} all-gather(bf16[16,512]{1,0:T(8,128)(2,1)S(1)} %get-tuple-element.3), channel_id=1, replica_groups=mesh['dp'=32,'tensor'=16] {'dp'}, dimensions={0}, use_global_device_ids=true | all-gather | bytes 540672 | tf_op jit(solution)/shard_map/all_gather | solution.py:54
  418.0 18.2 %all-reduce.3.cloned.1.call-done = bf16[512,512]{1,0:T(8,128)(2,1)} async-done(((bf16[512,512]{1,0:T(8,128)(2,1)}), bf16[512,512]{1,0:T(8,128)(2,1)}) %all-reduce.3.cloned.1.call-update) | async-done | bytes 524304 | tf_op jit(solution)/shard_map/psum | solution.py:19
  436.2 0.0 copy-done.2
  436.2 2.0 fusion.1
Async XLA Ops:
  8.0 1.2 copy-start
  8.0 356.3 %reduce-scatter.2.cloned.1.call-start = ((), (), s32[]{:S(2)}) async-start(), calls=%async_computation.2 | async-start | bytes 1081344 | tf_op jit(solution)/shard_map/reduce_scatter | solution.py:30
  215.3 3.4 copy-start.1
  218.6 145.7 %copy-start.3 = (f32[16,512]{1,0:T(8,128)S(1)}, f32[16,512]{1,0:T(8,128)}, u32[]{:S(2)}) copy-start(f32[16,512]{1,0:T(8,128)} %param.11) | copy-start | bytes 98308
  218.6 145.7 %copy-start.4 = (f32[16,512]{1,0:T(8,128)S(1)}, f32[16,512]{1,0:T(8,128)}, u32[]{:S(2)}) copy-start(f32[16,512]{1,0:T(8,128)} %param.10) | copy-start | bytes 98308
  218.6 217.7 %copy-start.2 = (bf16[256,512]{1,0:T(8,128)(2,1)S(1)}, bf16[256,512]{1,0:T(8,128)(2,1)}, u32[]{:S(2)}) copy-start(bf16[256,512]{1,0:T(8,128)(2,1)} %param.9) | copy-start | bytes 786436
  218.6 217.7 %all-reduce.3.cloned.1.call-start = ((), (), s32[]{:S(2)}) async-start(), calls=%async_computation.1 | async-start | bytes 1048576 | tf_op jit(solution)/shard_map/psum | solution.py:19
Sparse Core Ops, SparseCore 0:
  218.7 145.5 reduce-scatter.1
Sparse Core Ops, SparseCore 1:
  222.0 214.2 all-reduce.2
where the time goes:
time: 446 us
  blocking collectives  257 us (58%)
  waiting for transfers between devices  163 us (37%)
  between operations  15.5 us (3%)
  matrix products  6.99 us (2%)
    psum x1, blocking collectives, on_device(): projected = lax.psum(partial_sum, 'tensor').astype(jnp.bfloat16)  204 us
    reduce_scatter x1, waiting for transfers between devices, on_device(): lax.psum_scatter(lax.dot_general(columns, cotangent, (((0,), (0,)), ((),...  145 us
    all_gather x1, blocking collectives, on_device(): segment = lax.all_gather(update, 'dp', axis=0, tiled=True)  52.3 us
    psum x1, waiting for transfers between devices, broadcast(): return lax.psum(kept, axis)  18.2 us
  transfers between devices with their start and end apart: 2, of which 2 were waited for; matrix products, arithmetic and copies ran while one was open for 0% of the time, Pallas kernels for 0%

commit v1 on v0

v1 whole, which is shorter than its diff:
```python
import math

import jax
import jax.numpy as jnp
from jax import lax
from jax.sharding import Mesh, PartitionSpec as P

STEP = 1000


beta_one = 0.9
beta_two = 0.999
epsilon = 1e-08
step_size = 0.5

DATA = ("zl", "x", "core")
MODEL = ("zh", "y")
SIZES = {"zl": 4, "x": 4, "core": 2, "zh": 4, "y": 4}
bf16 = jnp.bfloat16
f32 = jnp.float32


def exchange(parts, axis):
    return lax.all_to_all(parts, axis, 0, 0)


def spread(block, axis, count):
    return exchange(jnp.broadcast_to(block[None], (count,) + block.shape), axis)


def basis_rows(projector, rows):
    half = lax.dynamic_slice_in_dim(projector, lax.axis_index("core") * rows, rows, 0)
    pairs = []
    for zl in range(4):
        for x in range(4):
            for core in range(2):
                for zh in range(4):
                    for y in range(4):
                        source = (((zl * 4 + x) * 2 + core) * 4 + zh) * 4 + y
                        target = (((zh * 4 + y) * 2 + core) * 4 + zl) * 4 + x
                        pairs.append((source, target))
    return lax.ppermute(half, DATA + MODEL, pairs)


def on_device(inputs, cotangent, projector, weight, moment, second_moment):
    tokens, width = inputs.shape[0], cotangent.shape[1]
    rank = projector.shape[1]
    rows = weight.shape[0]
    own_rows = basis_rows(projector, rows)

    partial_sum = jnp.dot(inputs, projector, preferred_element_type=f32).astype(bf16)
    parts = exchange(partial_sum.reshape(4, tokens // 4, rank), "y")
    half_sum = jnp.sum(parts.astype(f32), axis=0).astype(bf16)
    parts = exchange(half_sum.reshape(4, tokens // 16, rank), "zh")
    owned = jnp.sum(parts.astype(f32), axis=0).astype(bf16)
    quarter = spread(owned, "zh", 4).reshape(tokens // 4, rank)
    projected = spread(quarter, "y", 4).reshape(tokens, rank)

    scale = 1.0 / math.sqrt(tokens * 32)
    partial_gradient = lax.dot_general(
        projected, cotangent, (((0,), (0,)), ((), ())), preferred_element_type=f32
    ).astype(bf16)
    parts = exchange(partial_gradient.reshape(32, rank // 32, width), DATA)
    gradient = jnp.sum(parts.astype(f32), axis=0) * scale
    new_moment = beta_one * moment + (1.0 - beta_one) * gradient
    new_second = beta_two * second_moment + (1.0 - beta_two) * gradient * gradient
    first_fix = 1.0 - beta_one**STEP
    second_fix = 1.0 - beta_two**STEP
    update = (new_moment / first_fix / (jnp.sqrt(new_second / second_fix) + epsilon)).astype(bf16)
    segment = spread(update, DATA, 32).reshape(rank, width)
    expanded = jnp.dot(own_rows, segment, preferred_element_type=f32)
    new_weight = (weight.astype(f32) - step_size * expanded).astype(bf16)
    return (new_weight, new_moment, new_second)


def solution(mesh):
    names = DATA + MODEL
    fine = Mesh(mesh.devices.reshape([SIZES[name] for name in names]), names)
    split = P(DATA, MODEL)
    return jax.shard_map(
        on_device,
        mesh=fine,
        in_specs=(split, split, P(MODEL, None), split, split, split),
        out_specs=(split, split, split),
        check_vma=False,
    )
```

time: 446 us -> 162 us (0.36)
  the two profiles are of different devices: /device:TPU:6 before, /device:TPU:408 now
where the time goes in v1:
time: 162 us
  blocking collectives  102 us (63%)
  waiting for transfers between devices  35.1 us (22%)
  starting transfers between devices  17.6 us (11%)
  matrix products  3.47 us (2%)
  local copies, waits for them, and re-layouts  2.21 us (1%)
    all_to_all x5, blocking collectives, exchange(): return lax.all_to_all(parts, axis, 0, 0)  102 us
    ppermute x1, waiting for transfers between devices, basis_rows(): return lax.ppermute(half, DATA + MODEL, pairs)  35.1 us
    ppermute x1, starting transfers between devices, basis_rows(): return lax.ppermute(half, DATA + MODEL, pairs)  13 us
    all_to_all x1, starting transfers between devices, exchange(): return lax.all_to_all(parts, axis, 0, 0)  4.58 us
  transfers between devices with their start and end apart: 2, of which 1 were waited for; matrix products, arithmetic and copies ran while one was open for 0% of the time, Pallas kernels for 0%

profile of v1, /device:TPU:408, one launch (start us, length us, event | category | flops | bytes accessed | tf_op | source)
XLA Modules:
  0.0 161.9 jit_solution(14222671905993858352)
XLA Ops:
  0.6 0.0 copy-start
  0.6 1.2 copy-done
  1.9 1.7 %convolution_convert_fusion = bf16[1024,512]{1,0:T(8,128)(2,1)S(1)} fusion(bf16[1024,512]{1,0:T(8,128)(2,1)S(1)} %copy-done, bf16[512,512]{1,0:T(8,128)(2,1)} %param.8), kind=kOutput, calls=%fused_computation | convolution fusion | flops 537395200 | bytes 2621440 | tf_op jit(solution)/shard_map/dot_general | solution.py:51
  3.6 17.5 %all_to_all.30 = bf16[4,256,512]{2,1,0:T(8,128)(2,1)S(1)} all-to-all(bf16[4,256,512]{2,1,0:T(8,128)(2,1)S(1)} %bitcast.16), channel_id=1, replica_groups=mesh['zl'=4,'x'=4,'core'=2,'zh'=4,'y'=4] {'y'}, dimensions={0} | all-to-all | bytes 2097152 | tf_op jit(solution)/shard_map/all_to_all | solution.py:24
  21.1 0.2 reduce_sum.33
  21.4 23.2 %all_to_all.31 = bf16[4,64,512]{2,1,0:T(8,128)(2,1)S(1)} all-to-all(bf16[4,64,512]{2,1,0:T(8,128)(2,1)S(1)} %bitcast.13), channel_id=1, replica_groups=mesh['zl'=4,'x'=4,'core'=2,'zh'=4,'y'=4] {'zh'}, dimensions={0} | all-to-all | bytes 524288 | tf_op jit(solution)/shard_map/all_to_all | solution.py:24
  44.6 21.9 %all_to_all.32 = bf16[4,64,512]{2,1,0:T(8,128)(2,1)S(1)} all-to-all(bf16[4,64,512]{2,1,0:T(8,128)(2,1)S(1)} %broadcast_in_dim.8), channel_id=1, replica_groups=mesh['zl'=4,'x'=4,'core'=2,'zh'=4,'y'=4] {'zh'}, dimensions={0} | all-to-all | bytes 524288 | tf_op jit(solution)/shard_map/all_to_all | solution.py:24
  66.5 0.1 broadcast_in_dim.10
  66.6 0.0 copy-start.5
  66.6 13.4 %all_to_all.33 = bf16[4,256,512]{2,1,0:T(8,128)(2,1)S(1)} all-to-all(bf16[4,256,512]{2,1,0:T(8,128)(2,1)S(1)} %broadcast_in_dim.10), channel_id=1, replica_groups=mesh['zl'=4,'x'=4,'core'=2,'zh'=4,'y'=4] {'y'}, dimensions={0} | all-to-all | bytes 2097152 | tf_op jit(solution)/shard_map/all_to_all | solution.py:24
  80.1 0.0 copy-done.5
  80.1 0.7 convolution_convert_fusion.1
  80.8 0.0 copy-start.3
  80.8 0.0 copy-start.4
  80.8 25.7 %all_to_all.34 = bf16[32,16,512]{2,1,0:T(8,128)(2,1)S(1)} all-to-all(bf16[32,16,512]{2,1,0:T(8,128)(2,1)S(1)} %bitcast.17), channel_id=1, replica_groups=mesh['zl'=4,'x'=4,'core'=2,'zh'=4,'y'=4] {'zl','x','core'}, dimensions={0} | all-to-all | bytes 1048576 | tf_op jit(solution)/shard_map/all_to_all | solution.py:24
  106.6 0.0 copy-start.2
  106.6 0.1 convert_reduce_fusion
  106.6 0.0 copy-done.3
  106.7 0.0 copy-done.4
  106.7 0.6 divide_convert_fusion
  107.3 0.0 copy-start.1
  107.3 0.8 broadcast_in_dim.22
  108.1 4.6 %all-to-all-start.5 = ((bf16[32,16,512]{2,1,0:T(8,128)(2,1)}), bf16[32,16,512]{2,1,0:T(8,128)(2,1)S(1)}, u32[]{:S(2)}, u32[]{:S(2)}) async-start(bf16[32,16,512]{2,1,0:T(8,128)(2,1)} %broadcast_in_dim.22), calls=%async_computation.5 | async-start | bytes 1048576 | tf_op jit(solution)/shard_map/all_to_all | solution.py:24
  112.7 0.0 copy-done.2
  112.8 13.0 %collective-permute-start = (bf16[256,512]{1,0:T(8,128)(2,1)S(1)}, bf16[256,512]{1,0:T(8,128)(2,1)S(1)}, u32[]{:S(2)}, u32[]{:S(2)}) collective-permute-start(bf16[256,512]{1,0:T(8,128)(2,1)S(1)} %constant_dynamic-slice_fusion), channel_id=1, source_target_pairs={{0,0},{1,32},{2,64},{3,96},{4,128},{5,160},{6,192},{7,224},{8,256}... | collective-permute-start | bytes 786440 | tf_op jit(solution)/shard_map/ppermute | solution.py:42
  125.8 35.1 %collective-permute-done = bf16[256,512]{1,0:T(8,128)(2,1)S(1)} collective-permute-done((bf16[256,512]{1,0:T(8,128)(2,1)S(1)}, bf16[256,512]{1,0:T(8,128)(2,1)S(1)}, u32[]{:S(2)}, u32[]{:S(2)}) %collective-permute-start) | collective-permute-done | bytes 262176 | tf_op jit(solution)/shard_map/ppermute | solution.py:42
  160.9 0.0 all-to-all-done.5
  160.9 0.0 copy-done.1
  160.9 1.0 fusion.1
  (3 shorter events, 0.1 us)
Async XLA Ops:
  0.6 1.2 copy-start
  66.6 13.5 %copy-start.5 = (bf16[1024,512]{1,0:T(8,128)(2,1)S(1)}, bf16[1024,512]{1,0:T(8,128)(2,1)}, u32[]{:S(2)}) copy-start(bf16[1024,512]{1,0:T(8,128)(2,1)} %param.7) | copy-start | bytes 3145732
  80.8 25.8 %copy-start.3 = (f32[16,512]{1,0:T(8,128)S(1)}, f32[16,512]{1,0:T(8,128)}, u32[]{:S(2)}) copy-start(f32[16,512]{1,0:T(8,128)} %param.11) | copy-start | bytes 98308
  80.8 25.8 %copy-start.4 = (f32[16,512]{1,0:T(8,128)S(1)}, f32[16,512]{1,0:T(8,128)}, u32[]{:S(2)}) copy-start(f32[16,512]{1,0:T(8,128)} %param.10) | copy-start | bytes 98308
  106.6 6.2 %copy-start.2 = (bf16[512,512]{1,0:T(8,128)(2,1)S(1)}, bf16[512,512]{1,0:T(8,128)(2,1)}, u32[]{:S(2)}) copy-start(bf16[512,512]{1,0:T(8,128)(2,1)} %param.8) | copy-start | bytes 1572868
  107.3 53.6 %copy-start.1 = (bf16[256,512]{1,0:T(8,128)(2,1)S(1)}, bf16[256,512]{1,0:T(8,128)(2,1)}, u32[]{:S(2)}) copy-start(bf16[256,512]{1,0:T(8,128)(2,1)} %param.9) | copy-start | bytes 786436
  108.1 52.8 %all-to-all-start.5 = ((bf16[32,16,512]{2,1,0:T(8,128)(2,1)}), bf16[32,16,512]{2,1,0:T(8,128)(2,1)S(1)}, u32[]{:S(2)}, u32[]{:S(2)}) async-start(bf16[32,16,512]{2,1,0:T(8,128)(2,1)} %broadcast_in_dim.22), calls=%async_computation.5 | async-start | bytes 1048576 | tf_op jit(solution)/shard_map/all_to_all | solution.py:24
  112.8 48.1 %collective-permute-start = (bf16[256,512]{1,0:T(8,128)(2,1)S(1)}, bf16[256,512]{1,0:T(8,128)(2,1)S(1)}, u32[]{:S(2)}, u32[]{:S(2)}) collective-permute-start(bf16[256,512]{1,0:T(8,128)(2,1)S(1)} %constant_dynamic-slice_fusion), channel_id=1, source_target_pairs={{0,0},{1,32},{2,64},{3,96},{4,128},{5,160},{6,192},{7,224},{8,256}... | collective-permute-start | bytes 786440 | tf_op jit(solution)/shard_map/ppermute | solution.py:42

commit v2 on v1

v2 whole, which is shorter than its diff:
```python
import math

import jax
import jax.numpy as jnp
from jax import lax
from jax.experimental.layout import Layout, with_layout_constraint
from jax.sharding import Mesh, PartitionSpec as P

STEP = 1000


beta_one = 0.9
beta_two = 0.999
epsilon = 1e-08
step_size = 0.5

DATA = ("zl", "x", "core")
PLANE = ("zl", "x")
MODEL = ("zh", "y")
SIZES = {"zl": 4, "x": 4, "core": 2, "zh": 4, "y": 4}
bf16 = jnp.bfloat16
f32 = jnp.float32


def exchange(parts, axis):
    return lax.all_to_all(parts, axis, 0, 0)


def spread(block, axis, count):
    return exchange(jnp.broadcast_to(block[None], (count,) + block.shape), axis)


def rowwise(array):
    return with_layout_constraint(array, Layout(major_to_minor=(0, 1)))


def total(parts):
    return jnp.sum(parts.astype(f32), axis=0)


def regrouped(projector):
    rank = projector.shape[1]
    new = lax.broadcasted_iota(jnp.int32, (rank, rank), 1)
    old = lax.broadcasted_iota(jnp.int32, (rank, rank), 0)
    source = ((new & 240) << 1) | ((new >> 8) << 4) | (new & 15)
    select = (old == source).astype(bf16)
    return jnp.dot(projector, select, preferred_element_type=f32).astype(bf16)


def basis_rows(basis, rows):
    half = lax.dynamic_slice_in_dim(basis, lax.axis_index("core") * rows, rows, 0)
    pairs = []
    for zl in range(4):
        for x in range(4):
            for core in range(2):
                for zh in range(4):
                    for y in range(4):
                        source = (((zl * 4 + x) * 2 + core) * 4 + zh) * 4 + y
                        target = (((zh * 4 + y) * 2 + core) * 4 + zl) * 4 + x
                        pairs.append((source, target))
    return lax.ppermute(half, DATA + MODEL, pairs)


def step(inputs, cotangent, projector, weight, moment, second_moment):
    tokens, width = inputs.shape[0], cotangent.shape[1]
    rank = projector.shape[1]
    rows = weight.shape[0]
    basis = regrouped(projector)
    own_rows = basis_rows(basis, rows)
    negative_rows = lax.optimization_barrier(-own_rows)

    partial_sum = rowwise(jnp.dot(inputs, basis, preferred_element_type=f32).astype(bf16))
    parts = exchange(partial_sum.reshape(4, tokens // 4, rank), "y")
    half_sum = total(parts).astype(bf16)
    parts = exchange(half_sum.reshape(4, tokens // 16, rank), "zh")
    owned = total(parts).astype(bf16)
    quarter = spread(owned, "zh", 4).reshape(tokens // 4, rank)
    projected = spread(quarter, "y", 4).reshape(tokens, rank)

    scale = 1.0 / math.sqrt(tokens * 32)
    partial_gradient = lax.dot_general(
        projected, cotangent, (((0,), (0,)), ((), ())), preferred_element_type=f32
    ).astype(bf16)
    parts = exchange(partial_gradient.reshape(2, rank // 2, width), "core")
    chip_gradient = total(parts).astype(bf16)
    parts = exchange(chip_gradient.reshape(16, rank // 32, width), PLANE)
    gradient = total(parts) * scale
    new_moment = beta_one * moment + (1.0 - beta_one) * gradient
    new_second = beta_two * second_moment + (1.0 - beta_two) * gradient * gradient
    first_fix = 1.0 - beta_one**STEP
    second_fix = 1.0 - beta_two**STEP
    update = (new_moment / first_fix / (jnp.sqrt(new_second / second_fix) + epsilon)).astype(bf16)
    segment = spread(update, PLANE, 16).reshape(rank // 2, width)
    segment = lax.all_gather(segment, "core", axis=0, tiled=True)
    negative = jnp.dot(negative_rows, segment, preferred_element_type=f32)
    new_weight = (weight.astype(f32) + step_size * negative).astype(bf16)
    return (new_weight, new_moment, new_second)


def solution(mesh):
    names = DATA + MODEL
    fine = Mesh(mesh.devices.reshape([SIZES[name] for name in names]), names)
    split = P(DATA, MODEL)
    return jax.shard_map(
        step,
        mesh=fine,
        in_specs=(split, split, P(MODEL, None), split, split, split),
        out_specs=(split, split, split),
        check_vma=False,
    )
```

time: 162 us -> 158 us (0.975)
  the two profiles are of different devices: /device:TPU:408 before, /device:TPU:103 now
where the time goes in v2:
time: 158 us; the launch traced here: 157 us
  blocking collectives  109 us (69%)
  waiting for transfers between devices  30 us (19%)
  starting transfers between devices  10.9 us (7%)
  matrix products  4.12 us (3%)
    all_to_all x6, blocking collectives, exchange(): return lax.all_to_all(parts, axis, 0, 0)  107 us
    ppermute x1, waiting for transfers between devices, basis_rows(): return lax.ppermute(half, DATA + MODEL, pairs)  30 us
    all_to_all x1, starting transfers between devices, exchange(): return lax.all_to_all(parts, axis, 0, 0)  7.22 us
    ppermute x1, starting transfers between devices, basis_rows(): return lax.ppermute(half, DATA + MODEL, pairs)  3.69 us
  transfers between devices with their start and end apart: 2, of which 1 were waited for; matrix products, arithmetic and copies ran while one was open for 0% of the time, Pallas kernels for 0%

profile of v2, /device:TPU:103, one launch (start us, length us, event | category | flops | bytes accessed | tf_op | source)
XLA Modules:
  0.0 157.0 jit_solution(7861245099665438991)
XLA Ops:
  0.6 0.0 copy-start
  0.7 1.6 %convolution_convert_fusion.1 = bf16[512,512]{1,0:T(8,128)(2,1)S(1)} fusion(bf16[512,512]{1,0:T(8,128)(2,1)} %param.8, s32[512]{0:T(512)S(1)} %fusion.7), kind=kOutput, calls=%fused_computation.1 | convolution fusion | flops 269221888 | bytes 1050624 | tf_op jit(solution)/shard_map/dot_general | solution.py:47
  2.3 0.0 copy-done
  2.3 0.7 convolution_convert_fusion
  3.0 18.2 %all_to_all.35 = bf16[4,256,512]{2,1,0:T(8,128)(2,1)S(1)} all-to-all(bf16[4,256,512]{2,1,0:T(8,128)(2,1)S(1)} %bitcast.22), channel_id=1, replica_groups=mesh['zl'=4,'x'=4,'core'=2,'zh'=4,'y'=4] {'y'}, dimensions={0} | all-to-all | bytes 2097152 | tf_op jit(solution)/shard_map/all_to_all | solution.py:26
  21.3 0.2 reduce_sum.45
  21.5 26.1 %all_to_all.36 = bf16[4,64,512]{2,1,0:T(8,128)(2,1)S(1)} all-to-all(bf16[4,64,512]{2,1,0:T(8,128)(2,1)S(1)} %bitcast.19), channel_id=1, replica_groups=mesh['zl'=4,'x'=4,'core'=2,'zh'=4,'y'=4] {'zh'}, dimensions={0} | all-to-all | bytes 524288 | tf_op jit(solution)/shard_map/all_to_all | solution.py:26
  47.7 18.4 %all_to_all.37 = bf16[4,64,512]{2,1,0:T(8,128)(2,1)S(1)} all-to-all(bf16[4,64,512]{2,1,0:T(8,128)(2,1)S(1)} %broadcast_in_dim.8), channel_id=1, replica_groups=mesh['zl'=4,'x'=4,'core'=2,'zh'=4,'y'=4] {'zh'}, dimensions={0} | all-to-all | bytes 524288 | tf_op jit(solution)/shard_map/all_to_all | solution.py:26
  66.1 0.1 broadcast_in_dim.10
  66.2 0.0 copy-start.3
  66.2 12.3 %all_to_all.38 = bf16[4,256,512]{2,1,0:T(8,128)(2,1)S(1)} all-to-all(bf16[4,256,512]{2,1,0:T(8,128)(2,1)S(1)} %broadcast_in_dim.10), channel_id=1, replica_groups=mesh['zl'=4,'x'=4,'core'=2,'zh'=4,'y'=4] {'y'}, dimensions={0} | all-to-all | bytes 2097152 | tf_op jit(solution)/shard_map/all_to_all | solution.py:26
  78.5 0.0 copy-done.3
  78.5 0.7 convolution_convert_fusion.2
  79.2 14.7 %all_to_all.39 = bf16[2,256,512]{2,1,0:T(8,128)(2,1)S(1)} all-to-all(bf16[2,256,512]{2,1,0:T(8,128)(2,1)S(1)} %bitcast.24), channel_id=1, replica_groups=mesh['zl'=4,'x'=4,'core'=2,'zh'=4,'y'=4] {'core'}, dimensions={0} | all-to-all | bytes 1048576 | tf_op jit(solution)/shard_map/all_to_all | solution.py:26
  93.9 0.0 copy-start.1
  93.9 0.0 copy-start.2
  93.9 0.1 reduce_sum.47
  94.0 16.9 %all_to_all.40 = bf16[16,16,512]{2,1,0:T(8,128)(2,1)S(1)} all-to-all(bf16[16,16,512]{2,1,0:T(8,128)(2,1)S(1)} %bitcast.23), channel_id=1, replica_groups=mesh['zl'=4,'x'=4,'core'=2,'zh'=4,'y'=4] {'zl','x'}, dimensions={0} | all-to-all | bytes 524288 | tf_op jit(solution)/shard_map/all_to_all | solution.py:26
  110.9 0.0 copy-done.1
  110.9 0.0 copy-done.2
  110.9 0.6 divide_convert_fusion
  111.5 0.7 broadcast_in_dim.22
  112.3 7.2 %all-to-all-start.6 = ((bf16[16,16,512]{2,1,0:T(8,128)(2,1)}), bf16[16,16,512]{2,1,0:T(8,128)(2,1)S(1)}, u32[]{:S(2)}, u32[]{:S(2)}) async-start(bf16[16,16,512]{2,1,0:T(8,128)(2,1)} %broadcast_in_dim.22), calls=%async_computation.6 | async-start | bytes 524288 | tf_op jit(solution)/shard_map/all_to_all | solution.py:26
  119.5 0.0 copy-start.4
  119.5 3.7 %collective-permute-start = (bf16[256,512]{0,1:T(8,128)(2,1)S(1)}, bf16[256,512]{0,1:T(8,128)(2,1)S(1)}, u32[]{:S(2)}, u32[]{:S(2)}) collective-permute-start(bf16[256,512]{0,1:T(8,128)(2,1)S(1)} %dynamic-slice_bitcast_fusion), channel_id=1, source_target_pairs={{0,0},{1,32},{2,64},{3,96},{4,128},{5,160},{6,192},{7,224},{8,256}... | collective-permute-start | bytes 786440 | tf_op jit(solution)/shard_map/ppermute | solution.py:61
  123.2 30.0 %collective-permute-done = bf16[256,512]{0,1:T(8,128)(2,1)S(1)} collective-permute-done((bf16[256,512]{0,1:T(8,128)(2,1)S(1)}, bf16[256,512]{0,1:T(8,128)(2,1)S(1)}, u32[]{:S(2)}, u32[]{:S(2)}) %collective-permute-start) | collective-permute-done | bytes 262176 | tf_op jit(solution)/shard_map/ppermute | solution.py:61
  153.3 0.0 all-to-all-done.6
  153.3 2.7 %all_gather.3 = bf16[512,512]{1,0:T(8,128)(2,1)S(1)} all-gather(bf16[256,512]{1,0:T(8,128)(2,1)S(1)} %bitcast.18), channel_id=1, replica_groups=mesh['zl'=4,'x'=4,'core'=2,'zh'=4,'y'=4] {'core'}, dimensions={0}, use_global_device_ids=true | all-gather | bytes 786432 | tf_op jit(solution)/shard_map/all_gather | solution.py:94
  156.0 0.0 copy-done.4
  156.0 1.0 fusion.1
  (6 shorter events, 0.2 us)
Async XLA Ops:
  0.6 1.7 %copy-start = (bf16[1024,512]{1,0:T(8,128)(2,1)S(1)}, bf16[1024,512]{1,0:T(8,128)(2,1)}, u32[]{:S(2)}) copy-start(bf16[1024,512]{1,0:T(8,128)(2,1)} %param.6) | copy-start | bytes 3145732
  66.2 12.3 %copy-start.3 = (bf16[1024,512]{1,0:T(8,128)(2,1)S(1)}, bf16[1024,512]{1,0:T(8,128)(2,1)}, u32[]{:S(2)}) copy-start(bf16[1024,512]{1,0:T(8,128)(2,1)} %param.7) | copy-start | bytes 3145732
  93.9 17.0 %copy-start.1 = (f32[16,512]{1,0:T(8,128)S(1)}, f32[16,512]{1,0:T(8,128)}, u32[]{:S(2)}) copy-start(f32[16,512]{1,0:T(8,128)} %param.11) | copy-start | bytes 98308
  93.9 17.0 %copy-start.2 = (f32[16,512]{1,0:T(8,128)S(1)}, f32[16,512]{1,0:T(8,128)}, u32[]{:S(2)}) copy-start(f32[16,512]{1,0:T(8,128)} %param.10) | copy-start | bytes 98308
  112.3 41.0 %all-to-all-start.6 = ((bf16[16,16,512]{2,1,0:T(8,128)(2,1)}), bf16[16,16,512]{2,1,0:T(8,128)(2,1)S(1)}, u32[]{:S(2)}, u32[]{:S(2)}) async-start(bf16[16,16,512]{2,1,0:T(8,128)(2,1)} %broadcast_in_dim.22), calls=%async_computation.6 | async-start | bytes 524288 | tf_op jit(solution)/shard_map/all_to_all | solution.py:26
  119.5 36.5 %copy-start.4 = (bf16[256,512]{1,0:T(8,128)(2,1)S(1)}, bf16[256,512]{1,0:T(8,128)(2,1)}, u32[]{:S(2)}) copy-start(bf16[256,512]{1,0:T(8,128)(2,1)} %param.9) | copy-start | bytes 786436
  119.5 33.7 %collective-permute-start = (bf16[256,512]{0,1:T(8,128)(2,1)S(1)}, bf16[256,512]{0,1:T(8,128)(2,1)S(1)}, u32[]{:S(2)}, u32[]{:S(2)}) collective-permute-start(bf16[256,512]{0,1:T(8,128)(2,1)S(1)} %dynamic-slice_bitcast_fusion), channel_id=1, source_target_pairs={{0,0},{1,32},{2,64},{3,96},{4,128},{5,160},{6,192},{7,224},{8,256}... | collective-permute-start | bytes 786440 | tf_op jit(solution)/shard_map/ppermute | solution.py:61

commit v3 on v2

--- a/solution.py
+++ b/solution.py
@@ -47,18 +47,31 @@
     return jnp.dot(projector, select, preferred_element_type=f32).astype(bf16)
 
 
-def basis_rows(basis, rows):
-    half = lax.dynamic_slice_in_dim(basis, lax.axis_index("core") * rows, rows, 0)
+HOPS = ((0, 2, 3, 1), (0, 2, 3, 1), (2, 0, 1, 3), (2, 0, 1, 3))
+
+
+def place(zl, x, core, zh, y):
+    return (((zl * 4 + x) * 2 + core) * 4 + zh) * 4 + y
+
+
+def moved(rows, source_of):
     pairs = []
     for zl in range(4):
         for x in range(4):
             for core in range(2):
                 for zh in range(4):
                     for y in range(4):
-                        source = (((zl * 4 + x) * 2 + core) * 4 + zh) * 4 + y
-                        target = (((zh * 4 + y) * 2 + core) * 4 + zl) * 4 + x
-                        pairs.append((source, target))
-    return lax.ppermute(half, DATA + MODEL, pairs)
+                        here = (zl, x, core, zh, y)
+                        pairs.append((place(*source_of(*here)), place(*here)))
+    return lax.optimization_barrier(-lax.ppermute(rows, DATA + MODEL, pairs))
+
+
+def basis_rows(basis, rows):
+    half = lax.dynamic_slice_in_dim(basis, lax.axis_index("core") * rows, rows, 0)
+    half = moved(half, lambda zl, x, core, zh, y: (HOPS[zl][zh], x, core, zl, y))
+    half = moved(half, lambda zl, x, core, zh, y: (zl, x, core, zh, (y - x) % 4))
+    half = moved(half, lambda zl, x, core, zh, y: (zl, (y - x) % 4, core, zh, y))
+    return half
 
 
 def step(inputs, cotangent, projector, weight, moment, second_moment):
@@ -66,8 +79,7 @@
     rank = projector.shape[1]
     rows = weight.shape[0]
     basis = regrouped(projector)
-    own_rows = basis_rows(basis, rows)
-    negative_rows = lax.optimization_barrier(-own_rows)
+    negative_rows = basis_rows(basis, rows)
 
     partial_sum = rowwise(jnp.dot(inputs, basis, preferred_element_type=f32).astype(bf16))
     parts = exchange(partial_sum.reshape(4, tokens // 4, rank), "y")

time: 158 us -> 164 us (1.038)
  the two profiles are of different devices: /device:TPU:103 before, /device:TPU:99 now
where the time goes in v3:
time: 164 us; the launch traced here: 163 us
  blocking collectives  119 us (73%)
  waiting for transfers between devices  23.2 us (14%)
  starting transfers between devices  14 us (9%)
  matrix products  4.11 us (3%)
    all_to_all x6, blocking collectives, exchange(): return lax.all_to_all(parts, axis, 0, 0)  107 us
    ppermute x3, waiting for transfers between devices, moved(): return lax.optimization_barrier(-lax.ppermute(rows, DATA + MODEL, pairs))  23.2 us
    all_gather x1, blocking collectives, step(): segment = lax.all_gather(segment, 'core', axis=0, tiled=True)  12 us
    ppermute x3, starting transfers between devices, moved(): return lax.optimization_barrier(-lax.ppermute(rows, DATA + MODEL, pairs))  7.03 us
    all_to_all x1, starting transfers between devices, exchange(): return lax.all_to_all(parts, axis, 0, 0)  7.02 us
  transfers between devices with their start and end apart: 4, of which 3 were waited for; matrix products, arithmetic and copies ran while one was open for 0% of the time, Pallas kernels for 0%

profile of v3, /device:TPU:99, one launch (start us, length us, event | category | flops | bytes accessed | tf_op | source)
XLA Modules:
  0.0 163.0 jit_solution(6310110793268477440)
XLA Ops:
  0.6 0.0 copy-start
  0.7 1.6 convolution_convert_fusion.1
  2.3 0.0 copy-done
  2.3 0.7 convolution_convert_fusion
  3.0 18.2 %all_to_all.35 = bf16[4,256,512]{2,1,0:T(8,128)(2,1)S(1)} all-to-all(bf16[4,256,512]{2,1,0:T(8,128)(2,1)S(1)} %bitcast.22), channel_id=1, replica_groups=mesh['zl'=4,'x'=4,'core'=2,'zh'=4,'y'=4] {'y'}, dimensions={0} | all-to-all | bytes 2097152 | tf_op jit(solution)/shard_map/all_to_all | solution.py:26
  21.3 0.2 reduce_sum.45
  21.5 26.1 %all_to_all.36 = bf16[4,64,512]{2,1,0:T(8,128)(2,1)S(1)} all-to-all(bf16[4,64,512]{2,1,0:T(8,128)(2,1)S(1)} %bitcast.19), channel_id=1, replica_groups=mesh['zl'=4,'x'=4,'core'=2,'zh'=4,'y'=4] {'zh'}, dimensions={0} | all-to-all | bytes 524288 | tf_op jit(solution)/shard_map/all_to_all | solution.py:26
  47.7 18.4 %all_to_all.37 = bf16[4,64,512]{2,1,0:T(8,128)(2,1)S(1)} all-to-all(bf16[4,64,512]{2,1,0:T(8,128)(2,1)S(1)} %broadcast_in_dim.8), channel_id=1, replica_groups=mesh['zl'=4,'x'=4,'core'=2,'zh'=4,'y'=4] {'zh'}, dimensions={0} | all-to-all | bytes 524288 | tf_op jit(solution)/shard_map/all_to_all | solution.py:26
  66.1 0.1 broadcast_in_dim.10
  66.2 0.0 copy-start.3
  66.2 12.3 %all_to_all.38 = bf16[4,256,512]{2,1,0:T(8,128)(2,1)S(1)} all-to-all(bf16[4,256,512]{2,1,0:T(8,128)(2,1)S(1)} %broadcast_in_dim.10), channel_id=1, replica_groups=mesh['zl'=4,'x'=4,'core'=2,'zh'=4,'y'=4] {'y'}, dimensions={0} | all-to-all | bytes 2097152 | tf_op jit(solution)/shard_map/all_to_all | solution.py:26
  78.5 0.0 copy-done.3
  78.5 0.7 convolution_convert_fusion.2
  79.2 14.6 %all_to_all.39 = bf16[2,256,512]{2,1,0:T(8,128)(2,1)S(1)} all-to-all(bf16[2,256,512]{2,1,0:T(8,128)(2,1)S(1)} %bitcast.24), channel_id=1, replica_groups=mesh['zl'=4,'x'=4,'core'=2,'zh'=4,'y'=4] {'core'}, dimensions={0} | all-to-all | bytes 1048576 | tf_op jit(solution)/shard_map/all_to_all | solution.py:26
  93.8 0.1 reduce_sum.47
  93.9 17.2 %all_to_all.40 = bf16[16,16,512]{2,1,0:T(8,128)(2,1)S(1)} all-to-all(bf16[16,16,512]{2,1,0:T(8,128)(2,1)S(1)} %bitcast.23), channel_id=1, replica_groups=mesh['zl'=4,'x'=4,'core'=2,'zh'=4,'y'=4] {'zl','x'}, dimensions={0} | all-to-all | bytes 524288 | tf_op jit(solution)/shard_map/all_to_all | solution.py:26
  111.1 0.0 copy-done.1
  111.1 0.0 copy-done.2
  111.2 0.6 divide_convert_fusion
  111.8 0.7 broadcast_in_dim.22
  112.5 7.0 %all-to-all-start.6 = ((bf16[16,16,512]{2,1,0:T(8,128)(2,1)}), bf16[16,16,512]{2,1,0:T(8,128)(2,1)S(1)}, u32[]{:S(2)}, u32[]{:S(2)}) async-start(bf16[16,16,512]{2,1,0:T(8,128)(2,1)} %broadcast_in_dim.22), calls=%async_computation.6 | async-start | bytes 524288 | tf_op jit(solution)/shard_map/all_to_all | solution.py:26
  119.6 1.9 %collective-permute-start = (bf16[256,512]{0,1:T(8,128)(2,1)S(1)}, bf16[256,512]{0,1:T(8,128)(2,1)S(1)}, u32[]{:S(2)}, u32[]{:S(2)}) collective-permute-start(bf16[256,512]{0,1:T(8,128)(2,1)S(1)} %dynamic-slice_bitcast_fusion), channel_id=1, source_target_pairs={{0,0},{1,1},{2,2},{3,3},{256,4},{257,5},{258,6},{259,7},{384,8},{3... | collective-permute-start | bytes 786440 | tf_op jit(solution)/shard_map/ppermute | solution.py:66
  121.5 11.1 %collective-permute-done = bf16[256,512]{0,1:T(8,128)(2,1)S(1)} collective-permute-done((bf16[256,512]{0,1:T(8,128)(2,1)S(1)}, bf16[256,512]{0,1:T(8,128)(2,1)S(1)}, u32[]{:S(2)}, u32[]{:S(2)}) %collective-permute-start) | collective-permute-done | bytes 262176 | tf_op jit(solution)/shard_map/ppermute | solution.py:66
  132.6 0.0 copy-start.4
  132.6 2.3 %collective-permute-start.1 = (bf16[256,512]{0,1:T(8,128)(2,1)S(1)}, bf16[256,512]{0,1:T(8,128)(2,1)S(1)}, u32[]{:S(2)}, u32[]{:S(2)}) collective-permute-start(bf16[256,512]{0,1:T(8,128)(2,1)S(1)} %neg.9), channel_id=1, source_target_pairs={{0,0},{1,1},{2,2},{3,3},{4,4},{5,5},{6,6},{7,7},{8,8},{9,9},{10,10... | collective-permute-start | bytes 786440 | tf_op jit(solution)/shard_map/ppermute | solution.py:66
  135.0 6.1 %collective-permute-done.1 = bf16[256,512]{0,1:T(8,128)(2,1)S(1)} collective-permute-done((bf16[256,512]{0,1:T(8,128)(2,1)S(1)}, bf16[256,512]{0,1:T(8,128)(2,1)S(1)}, u32[]{:S(2)}, u32[]{:S(2)}) %collective-permute-start.1) | collective-permute-done | bytes 262176 | tf_op jit(solution)/shard_map/ppermute | solution.py:66
  141.2 2.8 %collective-permute-start.2 = (bf16[256,512]{0,1:T(8,128)(2,1)S(1)}, bf16[256,512]{0,1:T(8,128)(2,1)S(1)}, u32[]{:S(2)}, u32[]{:S(2)}) collective-permute-start(bf16[256,512]{0,1:T(8,128)(2,1)S(1)} %neg.10), channel_id=1, source_target_pairs={{0,0},{33,1},{66,2},{99,3},{4,4},{37,5},{70,6},{103,7},{8,8},{41,9... | collective-permute-start | bytes 786440 | tf_op jit(solution)/shard_map/ppermute | solution.py:66
  143.9 6.0 %collective-permute-done.2 = bf16[256,512]{0,1:T(8,128)(2,1)S(1)} collective-permute-done((bf16[256,512]{0,1:T(8,128)(2,1)S(1)}, bf16[256,512]{0,1:T(8,128)(2,1)S(1)}, u32[]{:S(2)}, u32[]{:S(2)}) %collective-permute-start.2) | collective-permute-done | bytes 262176 | tf_op jit(solution)/shard_map/ppermute | solution.py:66
  150.0 0.0 all-to-all-done.6
  150.0 12.0 %all_gather.3 = bf16[512,512]{1,0:T(8,128)(2,1)S(1)} all-gather(bf16[256,512]{1,0:T(8,128)(2,1)S(1)} %bitcast.18), channel_id=1, replica_groups=mesh['zl'=4,'x'=4,'core'=2,'zh'=4,'y'=4] {'core'}, dimensions={0}, use_global_device_ids=true | all-gather | bytes 786432 | tf_op jit(solution)/shard_map/all_gather | solution.py:106
  162.0 0.0 copy-done.4
  162.0 1.0 fusion.1
  (10 shorter events, 0.3 us)
Async XLA Ops:
  0.6 1.7 %copy-start = (bf16[1024,512]{1,0:T(8,128)(2,1)S(1)}, bf16[1024,512]{1,0:T(8,128)(2,1)}, u32[]{:S(2)}) copy-start(bf16[1024,512]{1,0:T(8,128)(2,1)} %param.6) | copy-start | bytes 3145732
  66.2 12.3 %copy-start.3 = (bf16[1024,512]{1,0:T(8,128)(2,1)S(1)}, bf16[1024,512]{1,0:T(8,128)(2,1)}, u32[]{:S(2)}) copy-start(bf16[1024,512]{1,0:T(8,128)(2,1)} %param.7) | copy-start | bytes 3145732
  93.8 17.4 %copy-start.1 = (f32[16,512]{1,0:T(8,128)S(1)}, f32[16,512]{1,0:T(8,128)}, u32[]{:S(2)}) copy-start(f32[16,512]{1,0:T(8,128)} %param.11) | copy-start | bytes 98308
  93.8 17.4 %copy-start.2 = (f32[16,512]{1,0:T(8,128)S(1)}, f32[16,512]{1,0:T(8,128)}, u32[]{:S(2)}) copy-start(f32[16,512]{1,0:T(8,128)} %param.10) | copy-start | bytes 98308
  112.5 37.5 %all-to-all-start.6 = ((bf16[16,16,512]{2,1,0:T(8,128)(2,1)}), bf16[16,16,512]{2,1,0:T(8,128)(2,1)S(1)}, u32[]{:S(2)}, u32[]{:S(2)}) async-start(bf16[16,16,512]{2,1,0:T(8,128)(2,1)} %broadcast_in_dim.22), calls=%async_computation.6 | async-start | bytes 524288 | tf_op jit(solution)/shard_map/all_to_all | solution.py:26
  119.6 13.0 %collective-permute-start = (bf16[256,512]{0,1:T(8,128)(2,1)S(1)}, bf16[256,512]{0,1:T(8,128)(2,1)S(1)}, u32[]{:S(2)}, u32[]{:S(2)}) collective-permute-start(bf16[256,512]{0,1:T(8,128)(2,1)S(1)} %dynamic-slice_bitcast_fusion), channel_id=1, source_target_pairs={{0,0},{1,1},{2,2},{3,3},{256,4},{257,5},{258,6},{259,7},{384,8},{3... | collective-permute-start | bytes 786440 | tf_op jit(solution)/shard_map/ppermute | solution.py:66
  132.6 29.4 %copy-start.4 = (bf16[256,512]{1,0:T(8,128)(2,1)S(1)}, bf16[256,512]{1,0:T(8,128)(2,1)}, u32[]{:S(2)}) copy-start(bf16[256,512]{1,0:T(8,128)(2,1)} %param.9) | copy-start | bytes 786436
  132.6 8.5 %collective-permute-start.1 = (bf16[256,512]{0,1:T(8,128)(2,1)S(1)}, bf16[256,512]{0,1:T(8,128)(2,1)S(1)}, u32[]{:S(2)}, u32[]{:S(2)}) collective-permute-start(bf16[256,512]{0,1:T(8,128)(2,1)S(1)} %neg.9), channel_id=1, source_target_pairs={{0,0},{1,1},{2,2},{3,3},{4,4},{5,5},{6,6},{7,7},{8,8},{9,9},{10,10... | collective-permute-start | bytes 786440 | tf_op jit(solution)/shard_map/ppermute | solution.py:66
  141.2 8.8 %collective-permute-start.2 = (bf16[256,512]{0,1:T(8,128)(2,1)S(1)}, bf16[256,512]{0,1:T(8,128)(2,1)S(1)}, u32[]{:S(2)}, u32[]{:S(2)}) collective-permute-start(bf16[256,512]{0,1:T(8,128)(2,1)S(1)} %neg.10), channel_id=1, source_target_pairs={{0,0},{33,1},{66,2},{99,3},{4,4},{37,5},{70,6},{103,7},{8,8},{41,9... | collective-permute-start | bytes 786440 | tf_op jit(solution)/shard_map/ppermute | solution.py:66

commit v4 on v3

--- a/solution.py
+++ b/solution.py
@@ -38,6 +38,16 @@
     return jnp.sum(parts.astype(f32), axis=0)
 
 
+NEAR = (((0, 1), (1, 0), (2, 3), (3, 2)), ((0, 3), (3, 0), (1, 2), (2, 1)))
+
+
+def line_sum(piece, first):
+    for stage in range(2):
+        other = lax.ppermute(piece, "zh", NEAR[(first + stage) % 2])
+        piece = lax.optimization_barrier((piece.astype(f32) + other.astype(f32)).astype(bf16))
+    return piece
+
+
 def regrouped(projector):
     rank = projector.shape[1]
     new = lax.broadcasted_iota(jnp.int32, (rank, rank), 1)
@@ -63,15 +73,16 @@
                     for y in range(4):
                         here = (zl, x, core, zh, y)
                         pairs.append((place(*source_of(*here)), place(*here)))
-    return lax.optimization_barrier(-lax.ppermute(rows, DATA + MODEL, pairs))
+    return lax.ppermute(rows, DATA + MODEL, pairs)
 
 
 def basis_rows(basis, rows):
     half = lax.dynamic_slice_in_dim(basis, lax.axis_index("core") * rows, rows, 0)
-    half = moved(half, lambda zl, x, core, zh, y: (HOPS[zl][zh], x, core, zl, y))
     half = moved(half, lambda zl, x, core, zh, y: (zl, x, core, zh, (y - x) % 4))
-    half = moved(half, lambda zl, x, core, zh, y: (zl, (y - x) % 4, core, zh, y))
-    return half
+    half = lax.optimization_barrier(-half)
+    return moved(
+        half, lambda zl, x, core, zh, y: (HOPS[zl][zh], (y - x) % 4, core, zl, y)
+    )
 
 
 def step(inputs, cotangent, projector, weight, moment, second_moment):
@@ -83,10 +94,12 @@
 
     partial_sum = rowwise(jnp.dot(inputs, basis, preferred_element_type=f32).astype(bf16))
     parts = exchange(partial_sum.reshape(4, tokens // 4, rank), "y")
-    half_sum = total(parts).astype(bf16)
-    parts = exchange(half_sum.reshape(4, tokens // 16, rank), "zh")
-    owned = total(parts).astype(bf16)
-    quarter = spread(owned, "zh", 4).reshape(tokens // 4, rank)
+    pieces = []
+    for index in range(2):
+        piece = parts[:, index * (tokens // 8) : (index + 1) * (tokens // 8)]
+        piece = lax.optimization_barrier(total(piece).astype(bf16))
+        pieces.append(line_sum(piece, index))
+    quarter = jnp.concatenate(pieces)
     projected = spread(quarter, "y", 4).reshape(tokens, rank)
 
     scale = 1.0 / math.sqrt(tokens * 32)

time: 164 us -> 144 us (0.88)
  the two profiles are of different devices: /device:TPU:99 before, /device:TPU:98 now
where the time goes in v4:
time: 144 us
  blocking collectives  57.1 us (40%)
  starting transfers between devices  44.1 us (31%)
  waiting for transfers between devices  35.5 us (25%)
  matrix products  4.11 us (3%)
    all_to_all x4, blocking collectives, exchange(): return lax.all_to_all(parts, axis, 0, 0)  54.9 us
    ppermute x4, starting transfers between devices, line_sum(): other = lax.ppermute(piece, 'zh', NEAR[(first + stage) % 2])  28.3 us
    ppermute x2, waiting for transfers between devices, moved(): return lax.ppermute(rows, DATA + MODEL, pairs)  20.9 us
    ppermute x4, waiting for transfers between devices, line_sum(): other = lax.ppermute(piece, 'zh', NEAR[(first + stage) % 2])  14.6 us
    ppermute x2, starting transfers between devices, moved(): return lax.ppermute(rows, DATA + MODEL, pairs)  8.38 us
    all_to_all x1, starting transfers between devices, exchange(): return lax.all_to_all(parts, axis, 0, 0)  7.4 us
  transfers between devices with their start and end apart: 7, of which 5 were waited for; matrix products, arithmetic and copies ran while one was open for 0% of the time, Pallas kernels for 0%

profile of v4, /device:TPU:98, one launch (start us, length us, event | category | flops | bytes accessed | tf_op | source)
XLA Modules:
  0.0 143.7 jit_solution(8827154104692827665)
XLA Ops:
  0.6 0.0 copy-start
  0.7 1.6 %convolution_convert_fusion.1 = bf16[512,512]{1,0:T(8,128)(2,1)S(1)} fusion(bf16[512,512]{1,0:T(8,128)(2,1)} %param.8, s32[512]{0:T(512)S(1)} %fusion.7), kind=kOutput, calls=%fused_computation.1 | convolution fusion | flops 269221888 | bytes 1050624 | tf_op jit(solution)/shard_map/dot_general | solution.py:57
  2.3 0.0 copy-done
  2.3 0.7 convolution_convert_fusion
  3.0 19.4 %all_to_all.25 = bf16[4,256,512]{2,1,0:T(8,128)(2,1)S(1)} all-to-all(bf16[4,256,512]{2,1,0:T(8,128)(2,1)S(1)} %bitcast.18), channel_id=1, replica_groups=mesh['zl'=4,'x'=4,'core'=2,'zh'=4,'y'=4] {'y'}, dimensions={0} | all-to-all | bytes 2097152 | tf_op jit(solution)/shard_map/all_to_all | solution.py:26
  22.4 0.2 slice_reduce_fusion.1
  22.6 10.0 %collective-permute-start.4 = (bf16[128,512]{1,0:T(8,128)(2,1)S(1)}, bf16[128,512]{1,0:T(8,128)(2,1)S(1)}, u32[]{:S(2)}, u32[]{:S(2)}) collective-permute-start(bf16[128,512]{1,0:T(8,128)(2,1)S(1)} %get-tuple-element.4), channel_id=1, source_target_pairs={{0,12},{12,0},{4,8},{8,4},{1,13},{13,1},{5,9},{9,5},{2,14},{14,2},... | collective-permute-start | bytes 393224 | tf_op jit(solution)/shard_map/ppermute | solution.py:46
  32.7 5.5 %collective-permute-start.2 = (bf16[128,512]{1,0:T(8,128)(2,1)S(1)}, bf16[128,512]{1,0:T(8,128)(2,1)S(1)}, u32[]{:S(2)}, u32[]{:S(2)}) collective-permute-start(bf16[128,512]{1,0:T(8,128)(2,1)S(1)} %get-tuple-element.3), channel_id=1, source_target_pairs={{0,4},{4,0},{8,12},{12,8},{1,5},{5,1},{9,13},{13,9},{2,6},{6,2},{1... | collective-permute-start | bytes 393224 | tf_op jit(solution)/shard_map/ppermute | solution.py:46
  38.1 5.6 %collective-permute-done.4 = bf16[128,512]{1,0:T(8,128)(2,1)S(1)} collective-permute-done((bf16[128,512]{1,0:T(8,128)(2,1)S(1)}, bf16[128,512]{1,0:T(8,128)(2,1)S(1)}, u32[]{:S(2)}, u32[]{:S(2)}) %collective-permute-start.4) | collective-permute-done | bytes 131104 | tf_op jit(solution)/shard_map/ppermute | solution.py:46
  43.8 4.4 %collective-permute-start.5 = (bf16[128,512]{1,0:T(8,128)(2,1)S(1)}, bf16[128,512]{1,0:T(8,128)(2,1)S(1)}, u32[]{:S(2)}, u32[]{:S(2)}) collective-permute-start(bf16[128,512]{1,0:T(8,128)(2,1)S(1)} %add_convert_fusion.1), channel_id=1, source_target_pairs={{0,4},{4,0},{8,12},{12,8},{1,5},{5,1},{9,13},{13,9},{2,6},{6,2},{1... | collective-permute-start | bytes 393224 | tf_op jit(solution)/shard_map/ppermute | solution.py:46
  48.2 0.0 collective-permute-done.2
  48.2 8.4 %collective-permute-start.3 = (bf16[128,512]{1,0:T(8,128)(2,1)S(1)}, bf16[128,512]{1,0:T(8,128)(2,1)S(1)}, u32[]{:S(2)}, u32[]{:S(2)}) collective-permute-start(bf16[128,512]{1,0:T(8,128)(2,1)S(1)} %add_convert_fusion.3), channel_id=1, source_target_pairs={{0,12},{12,0},{4,8},{8,4},{1,13},{13,1},{5,9},{9,5},{2,14},{14,2},... | collective-permute-start | bytes 393224 | tf_op jit(solution)/shard_map/ppermute | solution.py:46
  56.6 2.6 %collective-permute-done.5 = bf16[128,512]{1,0:T(8,128)(2,1)S(1)} collective-permute-done((bf16[128,512]{1,0:T(8,128)(2,1)S(1)}, bf16[128,512]{1,0:T(8,128)(2,1)S(1)}, u32[]{:S(2)}, u32[]{:S(2)}) %collective-permute-start.5) | collective-permute-done | bytes 131104 | tf_op jit(solution)/shard_map/ppermute | solution.py:46
  59.2 6.4 %collective-permute-done.3 = bf16[128,512]{1,0:T(8,128)(2,1)S(1)} collective-permute-done((bf16[128,512]{1,0:T(8,128)(2,1)S(1)}, bf16[128,512]{1,0:T(8,128)(2,1)S(1)}, u32[]{:S(2)}, u32[]{:S(2)}) %collective-permute-start.3) | collective-permute-done | bytes 131104 | tf_op jit(solution)/shard_map/ppermute | solution.py:46
  65.7 0.1 broadcast_in_dim.4
  65.8 0.0 copy-start.3
  65.8 16.0 %all_to_all.26 = bf16[4,256,512]{2,1,0:T(8,128)(2,1)S(1)} all-to-all(bf16[4,256,512]{2,1,0:T(8,128)(2,1)S(1)} %broadcast_in_dim.4), channel_id=1, replica_groups=mesh['zl'=4,'x'=4,'core'=2,'zh'=4,'y'=4] {'y'}, dimensions={0} | all-to-all | bytes 2097152 | tf_op jit(solution)/shard_map/all_to_all | solution.py:26
  81.8 0.7 convolution_convert_fusion.2
  82.5 4.2 %all_to_all.27 = bf16[2,256,512]{2,1,0:T(8,128)(2,1)S(1)} all-to-all(bf16[2,256,512]{2,1,0:T(8,128)(2,1)S(1)} %bitcast.20), channel_id=1, replica_groups=mesh['zl'=4,'x'=4,'core'=2,'zh'=4,'y'=4] {'core'}, dimensions={0} | all-to-all | bytes 1048576 | tf_op jit(solution)/shard_map/all_to_all | solution.py:26
  86.7 0.1 reduce_sum.47
  86.8 15.4 %all_to_all.28 = bf16[16,16,512]{2,1,0:T(8,128)(2,1)S(1)} all-to-all(bf16[16,16,512]{2,1,0:T(8,128)(2,1)S(1)} %bitcast.19), channel_id=1, replica_groups=mesh['zl'=4,'x'=4,'core'=2,'zh'=4,'y'=4] {'zl','x'}, dimensions={0} | all-to-all | bytes 524288 | tf_op jit(solution)/shard_map/all_to_all | solution.py:26
  102.3 0.6 divide_convert_fusion
  102.9 0.7 broadcast_in_dim.5
  103.6 7.4 %all-to-all-start.4 = ((bf16[16,16,512]{2,1,0:T(8,128)(2,1)}), bf16[16,16,512]{2,1,0:T(8,128)(2,1)S(1)}, u32[]{:S(2)}, u32[]{:S(2)}) async-start(bf16[16,16,512]{2,1,0:T(8,128)(2,1)} %broadcast_in_dim.5), calls=%async_computation.4 | async-start | bytes 524288 | tf_op jit(solution)/shard_map/all_to_all | solution.py:26
  111.1 2.6 %collective-permute-start = (bf16[256,512]{0,1:T(8,128)(2,1)S(1)}, bf16[256,512]{0,1:T(8,128)(2,1)S(1)}, u32[]{:S(2)}, u32[]{:S(2)}) collective-permute-start(bf16[256,512]{0,1:T(8,128)(2,1)S(1)} %dynamic-slice_bitcast_fusion), channel_id=1, source_target_pairs={{0,0},{1,1},{2,2},{3,3},{4,4},{5,5},{6,6},{7,7},{8,8},{9,9},{10,10... | collective-permute-start | bytes 786440 | tf_op jit(solution)/shard_map/ppermute | solution.py:76
  113.7 7.8 %collective-permute-done = bf16[256,512]{0,1:T(8,128)(2,1)S(1)} collective-permute-done((bf16[256,512]{0,1:T(8,128)(2,1)S(1)}, bf16[256,512]{0,1:T(8,128)(2,1)S(1)}, u32[]{:S(2)}, u32[]{:S(2)}) %collective-permute-start) | collective-permute-done | bytes 262176 | tf_op jit(solution)/shard_map/ppermute | solution.py:76
  121.5 5.8 %collective-permute-start.1 = (bf16[256,512]{0,1:T(8,128)(2,1)S(1)}, bf16[256,512]{0,1:T(8,128)(2,1)S(1)}, u32[]{:S(2)}, u32[]{:S(2)}) collective-permute-start(bf16[256,512]{0,1:T(8,128)(2,1)S(1)} %neg.3), channel_id=1, source_target_pairs={{0,0},{33,1},{66,2},{99,3},{256,4},{289,5},{322,6},{355,7},{384,8}... | collective-permute-start | bytes 786440 | tf_op jit(solution)/shard_map/ppermute | solution.py:76
  127.3 0.0 all-to-all-done.4
  127.3 2.2 %all_gather.3 = bf16[512,512]{1,0:T(8,128)(2,1)S(1)} all-gather(bf16[256,512]{1,0:T(8,128)(2,1)S(1)} %bitcast.16), channel_id=1, replica_groups=mesh['zl'=4,'x'=4,'core'=2,'zh'=4,'y'=4] {'core'}, dimensions={0}, use_global_device_ids=true | all-gather | bytes 786432 | tf_op jit(solution)/shard_map/all_gather | solution.py:119
  129.5 13.1 %collective-permute-done.1 = bf16[256,512]{0,1:T(8,128)(2,1)S(1)} collective-permute-done((bf16[256,512]{0,1:T(8,128)(2,1)S(1)}, bf16[256,512]{0,1:T(8,128)(2,1)S(1)}, u32[]{:S(2)}, u32[]{:S(2)}) %collective-permute-start.1) | collective-permute-done | bytes 262176 | tf_op jit(solution)/shard_map/ppermute | solution.py:76
  142.6 0.0 copy-done.4
  142.6 1.0 fusion.1
  (15 shorter events, 0.3 us)
Async XLA Ops:
  0.6 1.7 %copy-start = (bf16[1024,512]{1,0:T(8,128)(2,1)S(1)}, bf16[1024,512]{1,0:T(8,128)(2,1)}, u32[]{:S(2)}) copy-start(bf16[1024,512]{1,0:T(8,128)(2,1)} %param.6) | copy-start | bytes 3145732
  22.6 21.1 %collective-permute-start.4 = (bf16[128,512]{1,0:T(8,128)(2,1)S(1)}, bf16[128,512]{1,0:T(8,128)(2,1)S(1)}, u32[]{:S(2)}, u32[]{:S(2)}) collective-permute-start(bf16[128,512]{1,0:T(8,128)(2,1)S(1)} %get-tuple-element.4), channel_id=1, source_target_pairs={{0,12},{12,0},{4,8},{8,4},{1,13},{13,1},{5,9},{9,5},{2,14},{14,2},... | collective-permute-start | bytes 393224 | tf_op jit(solution)/shard_map/ppermute | solution.py:46
  32.7 15.5 %collective-permute-start.2 = (bf16[128,512]{1,0:T(8,128)(2,1)S(1)}, bf16[128,512]{1,0:T(8,128)(2,1)S(1)}, u32[]{:S(2)}, u32[]{:S(2)}) collective-permute-start(bf16[128,512]{1,0:T(8,128)(2,1)S(1)} %get-tuple-element.3), channel_id=1, source_target_pairs={{0,4},{4,0},{8,12},{12,8},{1,5},{5,1},{9,13},{13,9},{2,6},{6,2},{1... | collective-permute-start | bytes 393224 | tf_op jit(solution)/shard_map/ppermute | solution.py:46
  43.8 15.4 %collective-permute-start.5 = (bf16[128,512]{1,0:T(8,128)(2,1)S(1)}, bf16[128,512]{1,0:T(8,128)(2,1)S(1)}, u32[]{:S(2)}, u32[]{:S(2)}) collective-permute-start(bf16[128,512]{1,0:T(8,128)(2,1)S(1)} %add_convert_fusion.1), channel_id=1, source_target_pairs={{0,4},{4,0},{8,12},{12,8},{1,5},{5,1},{9,13},{13,9},{2,6},{6,2},{1... | collective-permute-start | bytes 393224 | tf_op jit(solution)/shard_map/ppermute | solution.py:46
  48.2 17.4 %collective-permute-start.3 = (bf16[128,512]{1,0:T(8,128)(2,1)S(1)}, bf16[128,512]{1,0:T(8,128)(2,1)S(1)}, u32[]{:S(2)}, u32[]{:S(2)}) collective-permute-start(bf16[128,512]{1,0:T(8,128)(2,1)S(1)} %add_convert_fusion.3), channel_id=1, source_target_pairs={{0,12},{12,0},{4,8},{8,4},{1,13},{13,1},{5,9},{9,5},{2,14},{14,2},... | collective-permute-start | bytes 393224 | tf_op jit(solution)/shard_map/ppermute | solution.py:46
  65.8 16.0 %copy-start.3 = (bf16[1024,512]{1,0:T(8,128)(2,1)S(1)}, bf16[1024,512]{1,0:T(8,128)(2,1)}, u32[]{:S(2)}) copy-start(bf16[1024,512]{1,0:T(8,128)(2,1)} %param.7) | copy-start | bytes 3145732
  86.7 15.6 %copy-start.1 = (f32[16,512]{1,0:T(8,128)S(1)}, f32[16,512]{1,0:T(8,128)}, u32[]{:S(2)}) copy-start(f32[16,512]{1,0:T(8,128)} %param.11) | copy-start | bytes 98308
  86.7 15.6 %copy-start.2 = (f32[16,512]{1,0:T(8,128)S(1)}, f32[16,512]{1,0:T(8,128)}, u32[]{:S(2)}) copy-start(f32[16,512]{1,0:T(8,128)} %param.10) | copy-start | bytes 98308
  103.6 23.7 %all-to-all-start.4 = ((bf16[16,16,512]{2,1,0:T(8,128)(2,1)}), bf16[16,16,512]{2,1,0:T(8,128)(2,1)S(1)}, u32[]{:S(2)}, u32[]{:S(2)}) async-start(bf16[16,16,512]{2,1,0:T(8,128)(2,1)} %broadcast_in_dim.5), calls=%async_computation.4 | async-start | bytes 524288 | tf_op jit(solution)/shard_map/all_to_all | solution.py:26
  111.0 31.6 %copy-start.4 = (bf16[256,512]{1,0:T(8,128)(2,1)S(1)}, bf16[256,512]{1,0:T(8,128)(2,1)}, u32[]{:S(2)}) copy-start(bf16[256,512]{1,0:T(8,128)(2,1)} %param.9) | copy-start | bytes 786436
  111.1 10.4 %collective-permute-start = (bf16[256,512]{0,1:T(8,128)(2,1)S(1)}, bf16[256,512]{0,1:T(8,128)(2,1)S(1)}, u32[]{:S(2)}, u32[]{:S(2)}) collective-permute-start(bf16[256,512]{0,1:T(8,128)(2,1)S(1)} %dynamic-slice_bitcast_fusion), channel_id=1, source_target_pairs={{0,0},{1,1},{2,2},{3,3},{4,4},{5,5},{6,6},{7,7},{8,8},{9,9},{10,10... | collective-permute-start | bytes 786440 | tf_op jit(solution)/shard_map/ppermute | solution.py:76
  121.5 21.1 %collective-permute-start.1 = (bf16[256,512]{0,1:T(8,128)(2,1)S(1)}, bf16[256,512]{0,1:T(8,128)(2,1)S(1)}, u32[]{:S(2)}, u32[]{:S(2)}) collective-permute-start(bf16[256,512]{0,1:T(8,128)(2,1)S(1)} %neg.3), channel_id=1, source_target_pairs={{0,0},{33,1},{66,2},{99,3},{256,4},{289,5},{322,6},{355,7},{384,8}... | collective-permute-start | bytes 786440 | tf_op jit(solution)/shard_map/ppermute | solution.py:76

commit v5 on v4

--- a/solution.py
+++ b/solution.py
@@ -76,8 +76,7 @@
     return lax.ppermute(rows, DATA + MODEL, pairs)
 
 
-def basis_rows(basis, rows):
-    half = lax.dynamic_slice_in_dim(basis, lax.axis_index("core") * rows, rows, 0)
+def basis_rows(half):
     half = moved(half, lambda zl, x, core, zh, y: (zl, x, core, zh, (y - x) % 4))
     half = lax.optimization_barrier(-half)
     return moved(
@@ -90,13 +89,16 @@
     rank = projector.shape[1]
     rows = weight.shape[0]
     basis = regrouped(projector)
-    negative_rows = basis_rows(basis, rows)
+    half = lax.dynamic_slice_in_dim(basis, lax.axis_index("core") * rows, rows, 0)
+    basis, half = lax.optimization_barrier((basis, half))
+    negative_rows = basis_rows(half)
 
     partial_sum = rowwise(jnp.dot(inputs, basis, preferred_element_type=f32).astype(bf16))
     parts = exchange(partial_sum.reshape(4, tokens // 4, rank), "y")
+    cuts = (0, 9 * (tokens // 64), tokens // 4)
     pieces = []
     for index in range(2):
-        piece = parts[:, index * (tokens // 8) : (index + 1) * (tokens // 8)]
+        piece = parts[:, cuts[index] : cuts[index + 1]]
         piece = lax.optimization_barrier(total(piece).astype(bf16))
         pieces.append(line_sum(piece, index))
     quarter = jnp.concatenate(pieces)

time: 144 us -> 146 us (1.014)
  waiting for transfers between devices: 35.5 us -> 41.8 us
  blocking collectives: 57.1 us -> 53.8 us
    ppermute x4, waiting for transfers between devices: 14.6 us -> 22 us  [line_sum(): other = lax.ppermute(piece, 'zh', NEAR[(first + stage) % 2])]
    all_to_all x4, blocking collectives: 54.9 us -> 51.6 us  [exchange(): return lax.all_to_all(parts, axis, 0, 0)]
    ppermute x4, starting transfers between devices: 28.3 us -> 26.1 us  [line_sum(): other = lax.ppermute(piece, 'zh', NEAR[(first + stage) % 2])]
where the time goes in v5:
time: 146 us; the launch traced here: 145 us
  blocking collectives  53.8 us (37%)
  starting transfers between devices  42.8 us (29%)
  waiting for transfers between devices  41.8 us (29%)
  matrix products  4.12 us (3%)
    all_to_all x4, blocking collectives, exchange(): return lax.all_to_all(parts, axis, 0, 0)  51.6 us
    ppermute x4, starting transfers between devices, line_sum(): other = lax.ppermute(piece, 'zh', NEAR[(first + stage) % 2])  26.1 us
    ppermute x4, waiting for transfers between devices, line_sum(): other = lax.ppermute(piece, 'zh', NEAR[(first + stage) % 2])  22 us
    ppermute x2, waiting for transfers between devices, moved(): return lax.ppermute(rows, DATA + MODEL, pairs)  19.8 us
    ppermute x2, starting transfers between devices, moved(): return lax.ppermute(rows, DATA + MODEL, pairs)  9.35 us
    all_to_all x1, starting transfers between devices, exchange(): return lax.all_to_all(parts, axis, 0, 0)  7.4 us
  transfers between devices with their start and end apart: 7, of which 5 were waited for; matrix products, arithmetic and copies ran while one was open for 0% of the time, Pallas kernels for 0%

profile of v5, /device:TPU:98, one launch (start us, length us, event | category | flops | bytes accessed | tf_op | source)
XLA Modules:
  0.0 145.4 jit_solution(5079115732315096922)
XLA Ops:
  0.6 0.0 copy-start
  0.7 1.6 %convolution_convert_fusion.1 = bf16[512,512]{1,0:T(8,128)(2,1)S(1)} fusion(bf16[512,512]{1,0:T(8,128)(2,1)} %param.8, s32[512]{0:T(512)S(1)} %fusion.7), kind=kOutput, calls=%fused_computation.1 | convolution fusion | flops 269221888 | bytes 1050624 | tf_op jit(solution)/shard_map/dot_general | solution.py:57
  2.3 0.0 copy-done
  2.3 0.7 convolution_convert_fusion
  3.1 19.4 %all_to_all.25 = bf16[4,256,512]{2,1,0:T(8,128)(2,1)S(1)} all-to-all(bf16[4,256,512]{2,1,0:T(8,128)(2,1)S(1)} %bitcast.18), channel_id=1, replica_groups=mesh['zl'=4,'x'=4,'core'=2,'zh'=4,'y'=4] {'y'}, dimensions={0} | all-to-all | bytes 2097152 | tf_op jit(solution)/shard_map/all_to_all | solution.py:26
  22.4 0.1 slice_reduce_fusion.1
  22.5 10.0 %collective-permute-start.4 = (bf16[112,512]{1,0:T(8,128)(2,1)S(1)}, bf16[112,512]{1,0:T(8,128)(2,1)S(1)}, u32[]{:S(2)}, u32[]{:S(2)}) collective-permute-start(bf16[112,512]{1,0:T(8,128)(2,1)S(1)} %slice_reduce_fusion.1), channel_id=1, source_target_pairs={{0,12},{12,0},{4,8},{8,4},{1,13},{13,1},{5,9},{9,5},{2,14},{14,2},... | collective-permute-start | bytes 344072 | tf_op jit(solution)/shard_map/ppermute | solution.py:46
  32.5 0.1 slice_reduce_fusion
  32.6 5.5 %collective-permute-start.2 = (bf16[144,512]{1,0:T(8,128)(2,1)S(1)}, bf16[144,512]{1,0:T(8,128)(2,1)S(1)}, u32[]{:S(2)}, u32[]{:S(2)}) collective-permute-start(bf16[144,512]{1,0:T(8,128)(2,1)S(1)} %slice_reduce_fusion), channel_id=1, source_target_pairs={{0,4},{4,0},{8,12},{12,8},{1,5},{5,1},{9,13},{13,9},{2,6},{6,2},{1... | collective-permute-start | bytes 442376 | tf_op jit(solution)/shard_map/ppermute | solution.py:46
  38.1 4.1 %collective-permute-done.4 = bf16[112,512]{1,0:T(8,128)(2,1)S(1)} collective-permute-done((bf16[112,512]{1,0:T(8,128)(2,1)S(1)}, bf16[112,512]{1,0:T(8,128)(2,1)S(1)}, u32[]{:S(2)}, u32[]{:S(2)}) %collective-permute-start.4) | collective-permute-done | bytes 114720 | tf_op jit(solution)/shard_map/ppermute | solution.py:46
  42.2 4.5 %collective-permute-start.5 = (bf16[112,512]{1,0:T(8,128)(2,1)S(1)}, bf16[112,512]{1,0:T(8,128)(2,1)S(1)}, u32[]{:S(2)}, u32[]{:S(2)}) collective-permute-start(bf16[112,512]{1,0:T(8,128)(2,1)S(1)} %add_convert_fusion.3), channel_id=1, source_target_pairs={{0,4},{4,0},{8,12},{12,8},{1,5},{5,1},{9,13},{13,9},{2,6},{6,2},{1... | collective-permute-start | bytes 344072 | tf_op jit(solution)/shard_map/ppermute | solution.py:46
  46.7 8.4 %collective-permute-done.2 = bf16[144,512]{1,0:T(8,128)(2,1)S(1)} collective-permute-done((bf16[144,512]{1,0:T(8,128)(2,1)S(1)}, bf16[144,512]{1,0:T(8,128)(2,1)S(1)}, u32[]{:S(2)}, u32[]{:S(2)}) %collective-permute-start.2) | collective-permute-done | bytes 147488 | tf_op jit(solution)/shard_map/ppermute | solution.py:46
  55.1 6.1 %collective-permute-start.3 = (bf16[144,512]{1,0:T(8,128)(2,1)S(1)}, bf16[144,512]{1,0:T(8,128)(2,1)S(1)}, u32[]{:S(2)}, u32[]{:S(2)}) collective-permute-start(bf16[144,512]{1,0:T(8,128)(2,1)S(1)} %add_convert_fusion.1), channel_id=1, source_target_pairs={{0,12},{12,0},{4,8},{8,4},{1,13},{13,1},{5,9},{9,5},{2,14},{14,2},... | collective-permute-start | bytes 442376 | tf_op jit(solution)/shard_map/ppermute | solution.py:46
  61.2 0.0 collective-permute-done.5
  61.3 9.5 %collective-permute-done.3 = bf16[144,512]{1,0:T(8,128)(2,1)S(1)} collective-permute-done((bf16[144,512]{1,0:T(8,128)(2,1)S(1)}, bf16[144,512]{1,0:T(8,128)(2,1)S(1)}, u32[]{:S(2)}, u32[]{:S(2)}) %collective-permute-start.3) | collective-permute-done | bytes 147488 | tf_op jit(solution)/shard_map/ppermute | solution.py:46
  70.9 0.1 broadcast_in_dim.4
  71.0 0.0 copy-start.3
  71.0 13.4 %all_to_all.26 = bf16[4,256,512]{2,1,0:T(8,128)(2,1)S(1)} all-to-all(bf16[4,256,512]{2,1,0:T(8,128)(2,1)S(1)} %broadcast_in_dim.4), channel_id=1, replica_groups=mesh['zl'=4,'x'=4,'core'=2,'zh'=4,'y'=4] {'y'}, dimensions={0} | all-to-all | bytes 2097152 | tf_op jit(solution)/shard_map/all_to_all | solution.py:26
  84.4 0.7 convolution_convert_fusion.2
  85.2 4.2 %all_to_all.27 = bf16[2,256,512]{2,1,0:T(8,128)(2,1)S(1)} all-to-all(bf16[2,256,512]{2,1,0:T(8,128)(2,1)S(1)} %bitcast.21), channel_id=1, replica_groups=mesh['zl'=4,'x'=4,'core'=2,'zh'=4,'y'=4] {'core'}, dimensions={0} | all-to-all | bytes 1048576 | tf_op jit(solution)/shard_map/all_to_all | solution.py:26
  89.3 0.1 reduce_sum.47
  89.4 14.7 %all_to_all.28 = bf16[16,16,512]{2,1,0:T(8,128)(2,1)S(1)} all-to-all(bf16[16,16,512]{2,1,0:T(8,128)(2,1)S(1)} %bitcast.20), channel_id=1, replica_groups=mesh['zl'=4,'x'=4,'core'=2,'zh'=4,'y'=4] {'zl','x'}, dimensions={0} | all-to-all | bytes 524288 | tf_op jit(solution)/shard_map/all_to_all | solution.py:26
  104.2 0.6 divide_convert_fusion
  104.8 0.7 broadcast_in_dim.5
  105.5 7.4 %all-to-all-start.4 = ((bf16[16,16,512]{2,1,0:T(8,128)(2,1)}), bf16[16,16,512]{2,1,0:T(8,128)(2,1)S(1)}, u32[]{:S(2)}, u32[]{:S(2)}) async-start(bf16[16,16,512]{2,1,0:T(8,128)(2,1)} %broadcast_in_dim.5), calls=%async_computation.4 | async-start | bytes 524288 | tf_op jit(solution)/shard_map/all_to_all | solution.py:26
  112.9 2.5 %collective-permute-start = (bf16[256,512]{0,1:T(8,128)(2,1)S(1)}, bf16[256,512]{0,1:T(8,128)(2,1)S(1)}, u32[]{:S(2)}, u32[]{:S(2)}) collective-permute-start(bf16[256,512]{0,1:T(8,128)(2,1)S(1)} %dynamic-slice_bitcast_fusion), channel_id=1, source_target_pairs={{0,0},{1,1},{2,2},{3,3},{4,4},{5,5},{6,6},{7,7},{8,8},{9,9},{10,10... | collective-permute-start | bytes 786440 | tf_op jit(solution)/shard_map/ppermute | solution.py:76
  115.4 7.8 %collective-permute-done = bf16[256,512]{0,1:T(8,128)(2,1)S(1)} collective-permute-done((bf16[256,512]{0,1:T(8,128)(2,1)S(1)}, bf16[256,512]{0,1:T(8,128)(2,1)S(1)}, u32[]{:S(2)}, u32[]{:S(2)}) %collective-permute-start) | collective-permute-done | bytes 262176 | tf_op jit(solution)/shard_map/ppermute | solution.py:76
  123.3 6.9 %collective-permute-start.1 = (bf16[256,512]{0,1:T(8,128)(2,1)S(1)}, bf16[256,512]{0,1:T(8,128)(2,1)S(1)}, u32[]{:S(2)}, u32[]{:S(2)}) collective-permute-start(bf16[256,512]{0,1:T(8,128)(2,1)S(1)} %neg.3), channel_id=1, source_target_pairs={{0,0},{33,1},{66,2},{99,3},{256,4},{289,5},{322,6},{355,7},{384,8}... | collective-permute-start | bytes 786440 | tf_op jit(solution)/shard_map/ppermute | solution.py:76
  130.1 0.0 all-to-all-done.4
  130.2 2.2 %all_gather.3 = bf16[512,512]{1,0:T(8,128)(2,1)S(1)} all-gather(bf16[256,512]{1,0:T(8,128)(2,1)S(1)} %bitcast.17), channel_id=1, replica_groups=mesh['zl'=4,'x'=4,'core'=2,'zh'=4,'y'=4] {'core'}, dimensions={0}, use_global_device_ids=true | all-gather | bytes 786432 | tf_op jit(solution)/shard_map/all_gather | solution.py:121
  132.3 12.0 %collective-permute-done.1 = bf16[256,512]{0,1:T(8,128)(2,1)S(1)} collective-permute-done((bf16[256,512]{0,1:T(8,128)(2,1)S(1)}, bf16[256,512]{0,1:T(8,128)(2,1)S(1)}, u32[]{:S(2)}, u32[]{:S(2)}) %collective-permute-start.1) | collective-permute-done | bytes 262176 | tf_op jit(solution)/shard_map/ppermute | solution.py:76
  144.3 1.0 fusion.1
  (16 shorter events, 0.3 us)
Async XLA Ops:
  0.6 1.7 %copy-start = (bf16[1024,512]{1,0:T(8,128)(2,1)S(1)}, bf16[1024,512]{1,0:T(8,128)(2,1)}, u32[]{:S(2)}) copy-start(bf16[1024,512]{1,0:T(8,128)(2,1)} %param.6) | copy-start | bytes 3145732
  22.5 19.7 %collective-permute-start.4 = (bf16[112,512]{1,0:T(8,128)(2,1)S(1)}, bf16[112,512]{1,0:T(8,128)(2,1)S(1)}, u32[]{:S(2)}, u32[]{:S(2)}) collective-permute-start(bf16[112,512]{1,0:T(8,128)(2,1)S(1)} %slice_reduce_fusion.1), channel_id=1, source_target_pairs={{0,12},{12,0},{4,8},{8,4},{1,13},{13,1},{5,9},{9,5},{2,14},{14,2},... | collective-permute-start | bytes 344072 | tf_op jit(solution)/shard_map/ppermute | solution.py:46
  32.6 22.4 %collective-permute-start.2 = (bf16[144,512]{1,0:T(8,128)(2,1)S(1)}, bf16[144,512]{1,0:T(8,128)(2,1)S(1)}, u32[]{:S(2)}, u32[]{:S(2)}) collective-permute-start(bf16[144,512]{1,0:T(8,128)(2,1)S(1)} %slice_reduce_fusion), channel_id=1, source_target_pairs={{0,4},{4,0},{8,12},{12,8},{1,5},{5,1},{9,13},{13,9},{2,6},{6,2},{1... | collective-permute-start | bytes 442376 | tf_op jit(solution)/shard_map/ppermute | solution.py:46
  42.2 19.0 %collective-permute-start.5 = (bf16[112,512]{1,0:T(8,128)(2,1)S(1)}, bf16[112,512]{1,0:T(8,128)(2,1)S(1)}, u32[]{:S(2)}, u32[]{:S(2)}) collective-permute-start(bf16[112,512]{1,0:T(8,128)(2,1)S(1)} %add_convert_fusion.3), channel_id=1, source_target_pairs={{0,4},{4,0},{8,12},{12,8},{1,5},{5,1},{9,13},{13,9},{2,6},{6,2},{1... | collective-permute-start | bytes 344072 | tf_op jit(solution)/shard_map/ppermute | solution.py:46
  55.1 15.7 %collective-permute-start.3 = (bf16[144,512]{1,0:T(8,128)(2,1)S(1)}, bf16[144,512]{1,0:T(8,128)(2,1)S(1)}, u32[]{:S(2)}, u32[]{:S(2)}) collective-permute-start(bf16[144,512]{1,0:T(8,128)(2,1)S(1)} %add_convert_fusion.1), channel_id=1, source_target_pairs={{0,12},{12,0},{4,8},{8,4},{1,13},{13,1},{5,9},{9,5},{2,14},{14,2},... | collective-permute-start | bytes 442376 | tf_op jit(solution)/shard_map/ppermute | solution.py:46
  71.0 13.5 %copy-start.3 = (bf16[1024,512]{1,0:T(8,128)(2,1)S(1)}, bf16[1024,512]{1,0:T(8,128)(2,1)}, u32[]{:S(2)}) copy-start(bf16[1024,512]{1,0:T(8,128)(2,1)} %param.7) | copy-start | bytes 3145732
  89.3 14.8 %copy-start.1 = (f32[16,512]{1,0:T(8,128)S(1)}, f32[16,512]{1,0:T(8,128)}, u32[]{:S(2)}) copy-start(f32[16,512]{1,0:T(8,128)} %param.11) | copy-start | bytes 98308
  89.3 14.8 %copy-start.2 = (f32[16,512]{1,0:T(8,128)S(1)}, f32[16,512]{1,0:T(8,128)}, u32[]{:S(2)}) copy-start(f32[16,512]{1,0:T(8,128)} %param.10) | copy-start | bytes 98308
  104.8 39.5 %copy-start.4 = (bf16[256,512]{1,0:T(8,128)(2,1)S(1)}, bf16[256,512]{1,0:T(8,128)(2,1)}, u32[]{:S(2)}) copy-start(bf16[256,512]{1,0:T(8,128)(2,1)} %param.9) | copy-start | bytes 786436
  105.5 24.6 %all-to-all-start.4 = ((bf16[16,16,512]{2,1,0:T(8,128)(2,1)}), bf16[16,16,512]{2,1,0:T(8,128)(2,1)S(1)}, u32[]{:S(2)}, u32[]{:S(2)}) async-start(bf16[16,16,512]{2,1,0:T(8,128)(2,1)} %broadcast_in_dim.5), calls=%async_computation.4 | async-start | bytes 524288 | tf_op jit(solution)/shard_map/all_to_all | solution.py:26
  112.9 10.3 %collective-permute-start = (bf16[256,512]{0,1:T(8,128)(2,1)S(1)}, bf16[256,512]{0,1:T(8,128)(2,1)S(1)}, u32[]{:S(2)}, u32[]{:S(2)}) collective-permute-start(bf16[256,512]{0,1:T(8,128)(2,1)S(1)} %dynamic-slice_bitcast_fusion), channel_id=1, source_target_pairs={{0,0},{1,1},{2,2},{3,3},{4,4},{5,5},{6,6},{7,7},{8,8},{9,9},{10,10... | collective-permute-start | bytes 786440 | tf_op jit(solution)/shard_map/ppermute | solution.py:76
  123.3 21.1 %collective-permute-start.1 = (bf16[256,512]{0,1:T(8,128)(2,1)S(1)}, bf16[256,512]{0,1:T(8,128)(2,1)S(1)}, u32[]{:S(2)}, u32[]{:S(2)}) collective-permute-start(bf16[256,512]{0,1:T(8,128)(2,1)S(1)} %neg.3), channel_id=1, source_target_pairs={{0,0},{33,1},{66,2},{99,3},{256,4},{289,5},{322,6},{355,7},{384,8}... | collective-permute-start | bytes 786440 | tf_op jit(solution)/shard_map/ppermute | solution.py:76

commit v6 on v5

--- a/solution.py
+++ b/solution.py
@@ -77,10 +77,10 @@
 
 
 def basis_rows(half):
-    half = moved(half, lambda zl, x, core, zh, y: (zl, x, core, zh, (y - x) % 4))
+    half = moved(half, lambda zl, x, core, zh, y: (zl, (y - x) % 4, core, zh, x))
     half = lax.optimization_barrier(-half)
     return moved(
-        half, lambda zl, x, core, zh, y: (HOPS[zl][zh], (y - x) % 4, core, zl, y)
+        half, lambda zl, x, core, zh, y: (HOPS[zl][zh], x, core, zl, y)
     )
 
 
@@ -95,7 +95,7 @@
 
     partial_sum = rowwise(jnp.dot(inputs, basis, preferred_element_type=f32).astype(bf16))
     parts = exchange(partial_sum.reshape(4, tokens // 4, rank), "y")
-    cuts = (0, 9 * (tokens // 64), tokens // 4)
+    cuts = (0, 17 * (tokens // 128), tokens // 4)
     pieces = []
     for index in range(2):
         piece = parts[:, cuts[index] : cuts[index + 1]]

time: 146 us -> 151 us (1.034)
  the two profiles are of different devices: /device:TPU:98 before, /device:TPU:56 now
where the time goes in v6:
time: 151 us; the launch traced here: 150 us
  blocking collectives  55.1 us (36%)
  waiting for transfers between devices  45.3 us (30%)
  starting transfers between devices  43 us (28%)
  matrix products  4.12 us (3%)
    all_to_all x4, blocking collectives, exchange(): return lax.all_to_all(parts, axis, 0, 0)  52.9 us
    ppermute x4, starting transfers between devices, line_sum(): other = lax.ppermute(piece, 'zh', NEAR[(first + stage) % 2])  25.5 us
    ppermute x2, waiting for transfers between devices, moved(): return lax.ppermute(rows, DATA + MODEL, pairs)  24.1 us
    ppermute x4, waiting for transfers between devices, line_sum(): other = lax.ppermute(piece, 'zh', NEAR[(first + stage) % 2])  21.2 us
    ppermute x2, starting transfers between devices, moved(): return lax.ppermute(rows, DATA + MODEL, pairs)  12.4 us
    all_to_all x1, starting transfers between devices, exchange(): return lax.all_to_all(parts, axis, 0, 0)  5.11 us
  transfers between devices with their start and end apart: 7, of which 5 were waited for; matrix products, arithmetic and copies ran while one was open for 0% of the time, Pallas kernels for 0%

profile of v6, /device:TPU:56, one launch (start us, length us, event | category | flops | bytes accessed | tf_op | source)
XLA Modules:
  0.0 150.4 jit_solution(2541339150684004951)
XLA Ops:
  0.6 0.0 copy-start
  0.7 1.6 %convolution_convert_fusion.1 = bf16[512,512]{1,0:T(8,128)(2,1)S(1)} fusion(bf16[512,512]{1,0:T(8,128)(2,1)} %param.8, s32[512]{0:T(512)S(1)} %fusion.7), kind=kOutput, calls=%fused_computation.1 | convolution fusion | flops 269221888 | bytes 1050624 | tf_op jit(solution)/shard_map/dot_general | solution.py:57
  2.3 0.7 convolution_convert_fusion
  3.1 17.5 %all_to_all.25 = bf16[4,256,512]{2,1,0:T(8,128)(2,1)S(1)} all-to-all(bf16[4,256,512]{2,1,0:T(8,128)(2,1)S(1)} %bitcast.18), channel_id=1, replica_groups=mesh['zl'=4,'x'=4,'core'=2,'zh'=4,'y'=4] {'y'}, dimensions={0} | all-to-all | bytes 2097152 | tf_op jit(solution)/shard_map/all_to_all | solution.py:26
  20.6 0.1 slice_reduce_fusion.1
  20.7 11.8 %collective-permute-start.4 = (bf16[120,512]{1,0:T(8,128)(2,1)S(1)}, bf16[120,512]{1,0:T(8,128)(2,1)S(1)}, u32[]{:S(2)}, u32[]{:S(2)}) collective-permute-start(bf16[120,512]{1,0:T(8,128)(2,1)S(1)} %slice_reduce_fusion.1), channel_id=1, source_target_pairs={{0,12},{12,0},{4,8},{8,4},{1,13},{13,1},{5,9},{9,5},{2,14},{14,2},... | collective-permute-start | bytes 368648 | tf_op jit(solution)/shard_map/ppermute | solution.py:46
  32.5 0.1 slice_reduce_fusion
  32.6 5.5 %collective-permute-start.2 = (bf16[136,512]{1,0:T(8,128)(2,1)S(1)}, bf16[136,512]{1,0:T(8,128)(2,1)S(1)}, u32[]{:S(2)}, u32[]{:S(2)}) collective-permute-start(bf16[136,512]{1,0:T(8,128)(2,1)S(1)} %slice_reduce_fusion), channel_id=1, source_target_pairs={{0,4},{4,0},{8,12},{12,8},{1,5},{5,1},{9,13},{13,9},{2,6},{6,2},{1... | collective-permute-start | bytes 417800 | tf_op jit(solution)/shard_map/ppermute | solution.py:46
  38.1 1.7 %collective-permute-done.4 = bf16[120,512]{1,0:T(8,128)(2,1)S(1)} collective-permute-done((bf16[120,512]{1,0:T(8,128)(2,1)S(1)}, bf16[120,512]{1,0:T(8,128)(2,1)S(1)}, u32[]{:S(2)}, u32[]{:S(2)}) %collective-permute-start.4) | collective-permute-done | bytes 122912 | tf_op jit(solution)/shard_map/ppermute | solution.py:46
  39.8 6.3 %collective-permute-start.5 = (bf16[120,512]{1,0:T(8,128)(2,1)S(1)}, bf16[120,512]{1,0:T(8,128)(2,1)S(1)}, u32[]{:S(2)}, u32[]{:S(2)}) collective-permute-start(bf16[120,512]{1,0:T(8,128)(2,1)S(1)} %add_convert_fusion.3), channel_id=1, source_target_pairs={{0,4},{4,0},{8,12},{12,8},{1,5},{5,1},{9,13},{13,9},{2,6},{6,2},{1... | collective-permute-start | bytes 368648 | tf_op jit(solution)/shard_map/ppermute | solution.py:46
  46.1 10.6 %collective-permute-done.2 = bf16[136,512]{1,0:T(8,128)(2,1)S(1)} collective-permute-done((bf16[136,512]{1,0:T(8,128)(2,1)S(1)}, bf16[136,512]{1,0:T(8,128)(2,1)S(1)}, u32[]{:S(2)}, u32[]{:S(2)}) %collective-permute-start.2) | collective-permute-done | bytes 139296 | tf_op jit(solution)/shard_map/ppermute | solution.py:46
  56.8 1.9 %collective-permute-start.3 = (bf16[136,512]{1,0:T(8,128)(2,1)S(1)}, bf16[136,512]{1,0:T(8,128)(2,1)S(1)}, u32[]{:S(2)}, u32[]{:S(2)}) collective-permute-start(bf16[136,512]{1,0:T(8,128)(2,1)S(1)} %add_convert_fusion.1), channel_id=1, source_target_pairs={{0,12},{12,0},{4,8},{8,4},{1,13},{13,1},{5,9},{9,5},{2,14},{14,2},... | collective-permute-start | bytes 417800 | tf_op jit(solution)/shard_map/ppermute | solution.py:46
  58.7 0.0 collective-permute-done.5
  58.8 8.9 %collective-permute-done.3 = bf16[136,512]{1,0:T(8,128)(2,1)S(1)} collective-permute-done((bf16[136,512]{1,0:T(8,128)(2,1)S(1)}, bf16[136,512]{1,0:T(8,128)(2,1)S(1)}, u32[]{:S(2)}, u32[]{:S(2)}) %collective-permute-start.3) | collective-permute-done | bytes 139296 | tf_op jit(solution)/shard_map/ppermute | solution.py:46
  67.7 0.1 broadcast_in_dim.4
  67.8 0.0 copy-start.3
  67.8 13.4 %all_to_all.26 = bf16[4,256,512]{2,1,0:T(8,128)(2,1)S(1)} all-to-all(bf16[4,256,512]{2,1,0:T(8,128)(2,1)S(1)} %broadcast_in_dim.4), channel_id=1, replica_groups=mesh['zl'=4,'x'=4,'core'=2,'zh'=4,'y'=4] {'y'}, dimensions={0} | all-to-all | bytes 2097152 | tf_op jit(solution)/shard_map/all_to_all | solution.py:26
  81.2 0.0 copy-done.3
  81.2 0.7 convolution_convert_fusion.2
  82.0 4.2 %all_to_all.27 = bf16[2,256,512]{2,1,0:T(8,128)(2,1)S(1)} all-to-all(bf16[2,256,512]{2,1,0:T(8,128)(2,1)S(1)} %bitcast.21), channel_id=1, replica_groups=mesh['zl'=4,'x'=4,'core'=2,'zh'=4,'y'=4] {'core'}, dimensions={0} | all-to-all | bytes 1048576 | tf_op jit(solution)/shard_map/all_to_all | solution.py:26
  86.1 0.1 reduce_sum.47
  86.2 17.8 %all_to_all.28 = bf16[16,16,512]{2,1,0:T(8,128)(2,1)S(1)} all-to-all(bf16[16,16,512]{2,1,0:T(8,128)(2,1)S(1)} %bitcast.20), channel_id=1, replica_groups=mesh['zl'=4,'x'=4,'core'=2,'zh'=4,'y'=4] {'zl','x'}, dimensions={0} | all-to-all | bytes 524288 | tf_op jit(solution)/shard_map/all_to_all | solution.py:26
  104.1 0.6 divide_convert_fusion
  104.7 0.7 broadcast_in_dim.5
  105.5 5.1 %all-to-all-start.4 = ((bf16[16,16,512]{2,1,0:T(8,128)(2,1)}), bf16[16,16,512]{2,1,0:T(8,128)(2,1)S(1)}, u32[]{:S(2)}, u32[]{:S(2)}) async-start(bf16[16,16,512]{2,1,0:T(8,128)(2,1)} %broadcast_in_dim.5), calls=%async_computation.4 | async-start | bytes 524288 | tf_op jit(solution)/shard_map/all_to_all | solution.py:26
  110.6 4.6 %collective-permute-start = (bf16[256,512]{0,1:T(8,128)(2,1)S(1)}, bf16[256,512]{0,1:T(8,128)(2,1)S(1)}, u32[]{:S(2)}, u32[]{:S(2)}) collective-permute-start(bf16[256,512]{0,1:T(8,128)(2,1)S(1)} %dynamic-slice_bitcast_fusion), channel_id=1, source_target_pairs={{0,0},{32,1},{64,2},{96,3},{4,4},{36,5},{68,6},{100,7},{8,8},{40,9... | collective-permute-start | bytes 786440 | tf_op jit(solution)/shard_map/ppermute | solution.py:76
  115.2 15.0 %collective-permute-done = bf16[256,512]{0,1:T(8,128)(2,1)S(1)} collective-permute-done((bf16[256,512]{0,1:T(8,128)(2,1)S(1)}, bf16[256,512]{0,1:T(8,128)(2,1)S(1)}, u32[]{:S(2)}, u32[]{:S(2)}) %collective-permute-start) | collective-permute-done | bytes 262176 | tf_op jit(solution)/shard_map/ppermute | solution.py:76
  130.2 7.8 %collective-permute-start.1 = (bf16[256,512]{0,1:T(8,128)(2,1)S(1)}, bf16[256,512]{0,1:T(8,128)(2,1)S(1)}, u32[]{:S(2)}, u32[]{:S(2)}) collective-permute-start(bf16[256,512]{0,1:T(8,128)(2,1)S(1)} %neg.3), channel_id=1, source_target_pairs={{0,0},{1,1},{2,2},{3,3},{256,4},{257,5},{258,6},{259,7},{384,8},{3... | collective-permute-start | bytes 786440 | tf_op jit(solution)/shard_map/ppermute | solution.py:76
  138.0 0.0 all-to-all-done.4
  138.0 2.2 %all_gather.3 = bf16[512,512]{1,0:T(8,128)(2,1)S(1)} all-gather(bf16[256,512]{1,0:T(8,128)(2,1)S(1)} %bitcast.17), channel_id=1, replica_groups=mesh['zl'=4,'x'=4,'core'=2,'zh'=4,'y'=4] {'core'}, dimensions={0}, use_global_device_ids=true | all-gather | bytes 786432 | tf_op jit(solution)/shard_map/all_gather | solution.py:121
  140.2 9.1 %collective-permute-done.1 = bf16[256,512]{0,1:T(8,128)(2,1)S(1)} collective-permute-done((bf16[256,512]{0,1:T(8,128)(2,1)S(1)}, bf16[256,512]{0,1:T(8,128)(2,1)S(1)}, u32[]{:S(2)}, u32[]{:S(2)}) %collective-permute-start.1) | collective-permute-done | bytes 262176 | tf_op jit(solution)/shard_map/ppermute | solution.py:76
  149.4 1.0 fusion.1
  (16 shorter events, 0.3 us)
Async XLA Ops:
  0.6 1.7 %copy-start = (bf16[1024,512]{1,0:T(8,128)(2,1)S(1)}, bf16[1024,512]{1,0:T(8,128)(2,1)}, u32[]{:S(2)}) copy-start(bf16[1024,512]{1,0:T(8,128)(2,1)} %param.6) | copy-start | bytes 3145732
  20.7 19.1 %collective-permute-start.4 = (bf16[120,512]{1,0:T(8,128)(2,1)S(1)}, bf16[120,512]{1,0:T(8,128)(2,1)S(1)}, u32[]{:S(2)}, u32[]{:S(2)}) collective-permute-start(bf16[120,512]{1,0:T(8,128)(2,1)S(1)} %slice_reduce_fusion.1), channel_id=1, source_target_pairs={{0,12},{12,0},{4,8},{8,4},{1,13},{13,1},{5,9},{9,5},{2,14},{14,2},... | collective-permute-start | bytes 368648 | tf_op jit(solution)/shard_map/ppermute | solution.py:46
  32.6 24.1 %collective-permute-start.2 = (bf16[136,512]{1,0:T(8,128)(2,1)S(1)}, bf16[136,512]{1,0:T(8,128)(2,1)S(1)}, u32[]{:S(2)}, u32[]{:S(2)}) collective-permute-start(bf16[136,512]{1,0:T(8,128)(2,1)S(1)} %slice_reduce_fusion), channel_id=1, source_target_pairs={{0,4},{4,0},{8,12},{12,8},{1,5},{5,1},{9,13},{13,9},{2,6},{6,2},{1... | collective-permute-start | bytes 417800 | tf_op jit(solution)/shard_map/ppermute | solution.py:46
  39.8 18.9 %collective-permute-start.5 = (bf16[120,512]{1,0:T(8,128)(2,1)S(1)}, bf16[120,512]{1,0:T(8,128)(2,1)S(1)}, u32[]{:S(2)}, u32[]{:S(2)}) collective-permute-start(bf16[120,512]{1,0:T(8,128)(2,1)S(1)} %add_convert_fusion.3), channel_id=1, source_target_pairs={{0,4},{4,0},{8,12},{12,8},{1,5},{5,1},{9,13},{13,9},{2,6},{6,2},{1... | collective-permute-start | bytes 368648 | tf_op jit(solution)/shard_map/ppermute | solution.py:46
  56.8 10.9 %collective-permute-start.3 = (bf16[136,512]{1,0:T(8,128)(2,1)S(1)}, bf16[136,512]{1,0:T(8,128)(2,1)S(1)}, u32[]{:S(2)}, u32[]{:S(2)}) collective-permute-start(bf16[136,512]{1,0:T(8,128)(2,1)S(1)} %add_convert_fusion.1), channel_id=1, source_target_pairs={{0,12},{12,0},{4,8},{8,4},{1,13},{13,1},{5,9},{9,5},{2,14},{14,2},... | collective-permute-start | bytes 417800 | tf_op jit(solution)/shard_map/ppermute | solution.py:46
  67.8 13.5 %copy-start.3 = (bf16[1024,512]{1,0:T(8,128)(2,1)S(1)}, bf16[1024,512]{1,0:T(8,128)(2,1)}, u32[]{:S(2)}) copy-start(bf16[1024,512]{1,0:T(8,128)(2,1)} %param.7) | copy-start | bytes 3145732
  86.1 18.0 %copy-start.1 = (f32[16,512]{1,0:T(8,128)S(1)}, f32[16,512]{1,0:T(8,128)}, u32[]{:S(2)}) copy-start(f32[16,512]{1,0:T(8,128)} %param.11) | copy-start | bytes 98308
  86.1 18.0 %copy-start.2 = (f32[16,512]{1,0:T(8,128)S(1)}, f32[16,512]{1,0:T(8,128)}, u32[]{:S(2)}) copy-start(f32[16,512]{1,0:T(8,128)} %param.10) | copy-start | bytes 98308
  104.7 44.6 %copy-start.4 = (bf16[256,512]{1,0:T(8,128)(2,1)S(1)}, bf16[256,512]{1,0:T(8,128)(2,1)}, u32[]{:S(2)}) copy-start(bf16[256,512]{1,0:T(8,128)(2,1)} %param.9) | copy-start | bytes 786436
  105.5 32.6 %all-to-all-start.4 = ((bf16[16,16,512]{2,1,0:T(8,128)(2,1)}), bf16[16,16,512]{2,1,0:T(8,128)(2,1)S(1)}, u32[]{:S(2)}, u32[]{:S(2)}) async-start(bf16[16,16,512]{2,1,0:T(8,128)(2,1)} %broadcast_in_dim.5), calls=%async_computation.4 | async-start | bytes 524288 | tf_op jit(solution)/shard_map/all_to_all | solution.py:26
  110.6 19.6 %collective-permute-start = (bf16[256,512]{0,1:T(8,128)(2,1)S(1)}, bf16[256,512]{0,1:T(8,128)(2,1)S(1)}, u32[]{:S(2)}, u32[]{:S(2)}) collective-permute-start(bf16[256,512]{0,1:T(8,128)(2,1)S(1)} %dynamic-slice_bitcast_fusion), channel_id=1, source_target_pairs={{0,0},{32,1},{64,2},{96,3},{4,4},{36,5},{68,6},{100,7},{8,8},{40,9... | collective-permute-start | bytes 786440 | tf_op jit(solution)/shard_map/ppermute | solution.py:76
  130.2 19.2 %collective-permute-start.1 = (bf16[256,512]{0,1:T(8,128)(2,1)S(1)}, bf16[256,512]{0,1:T(8,128)(2,1)S(1)}, u32[]{:S(2)}, u32[]{:S(2)}) collective-permute-start(bf16[256,512]{0,1:T(8,128)(2,1)S(1)} %neg.3), channel_id=1, source_target_pairs={{0,0},{1,1},{2,2},{3,3},{256,4},{257,5},{258,6},{259,7},{384,8},{3... | collective-permute-start | bytes 786440 | tf_op jit(solution)/shard_map/ppermute | solution.py:76
